TPU v7x, 32 devices: a whole 2x2x4 slice. The times are simulated.
32 devices in a mesh: dp: 4 (over y, x), mp: 8 (over z, core).
Axes of the slice: x: 2, y: 2, z: 4, core: 2. Of those that a mesh axis runs over, the one named last changes fastest.
Arguments:
- tokens: bfloat16 [8192, 2048], P(('dp', 'mp')), may hold values from -6 to 6
- ln1_gain: float32 [2048], replicated, may hold values from 0.5 to 1.5
- ln1_bias: float32 [2048], replicated, may hold values from -1.75 to 1.75
- w_query: bfloat16 [2048, 2048], P(None, 'mp'), may hold values from -0.125 to 0.125
- b_query: float32 [2048], P('mp'), may hold values from -3 to 3
- w_key: bfloat16 [2048, 2048], P(None, 'mp'), may hold values from -0.125 to 0.125
- w_value: bfloat16 [2048, 2048], P(None, 'mp'), may hold values from -0.125 to 0.125
- b_value: float32 [2048], P('mp'), may hold values from -0.125 to 0.125
- w_out: bfloat16 [2048, 2048], P('mp'), may hold values from -2 to 2
- b_out: float32 [2048], replicated, may hold values from -3 to 3
- ln2_gain: float32 [2048], replicated, may hold values from 0.5 to 1.5
- ln2_bias: float32 [2048], replicated, may hold values from -1.75 to 1.75
- w_up: bfloat16 [2048, 8192], P(None, 'mp'), may hold values from -0.125 to 0.125
- b_up: float32 [8192], P('mp'), may hold values from -3 to 3
- w_down: bfloat16 [8192, 2048], P('mp'), may hold values from -0.0625 to 0.0625
- b_down: float32 [2048], replicated, may hold values from -3 to 3
- cotangent: bfloat16 [8192, 2048], P(('dp', 'mp')), may hold values from -6 to 6
- seq_ids: int32 [4, 2048], P('dp'), may hold values from 0 to 2, as said below
- block_mask: int32 [4, 8, 8], P('dp'), may hold values from 0 to 1, as said below
- counts: int32 [4], replicated, may hold values from 512 to 2048, as said below
Outputs:
- output: float32 [8192, 2048], P(('dp', 'mp'))
- grad_in: float32 [8192, 2048], P(('dp', 'mp'))
- grad_ln1_gain: float32 [2048], replicated
- grad_ln1_bias: float32 [2048], replicated
- grad_w_query: float32 [2048, 2048], P(None, 'mp')
- grad_b_query: float32 [2048], P('mp')
- grad_w_key: float32 [2048, 2048], P(None, 'mp')
- grad_w_value: float32 [2048, 2048], P(None, 'mp')
- grad_b_value: float32 [2048], P('mp')
- grad_w_out: float32 [2048, 2048], P('mp')
- grad_b_out: float32 [2048], replicated
- grad_ln2_gain: float32 [2048], replicated
- grad_ln2_bias: float32 [2048], replicated
- grad_w_up: float32 [2048, 8192], P(None, 'mp')
- grad_b_up: float32 [8192], P('mp')
- grad_w_down: float32 [8192, 2048], P('mp')
- grad_b_down: float32 [2048], replicated
Inputs may be any that keep to these rules, and one draw needn't show every extreme that they name: `counts`: one group's count equals 2048 in every draw. `seq_ids`: in group g, slots before a cut carry 0, slots from the cut up to counts[g] - 1 carry 1, later slots carry 2; the cut lies between max(counts[g] - 2048, counts[g] // 2) and min(counts[g], 2048). `block_mask`: diagonal entries are 1 and entries above the diagonal are 0.
All inputs are finite; a program needn't handle non-finite values.
Results may differ from a plain program's by a relative error of at most 0.012.
Values may be sent and summed in bfloat16 or wider, within the bound.
No kernel may reach another device: no remote copies, remote signals or barrier semaphores. Data moves between devices by JAX's collectives and lax.ppermute only.
A program may use at most 256 MiB of HBM per device.

v0:
```python
import jax
import jax.numpy as jnp
from jax import lax
from jax.sharding import PartitionSpec as P

HD = 128
BLOCK = 256


epsilon = 1e-05


def layer_norm(values, gain, bias):
    average = jnp.mean(values, axis=-1, keepdims=True)
    centered = values - average
    variance = jnp.mean(centered * centered, axis=-1, keepdims=True)
    return centered * lax.rsqrt(variance + epsilon) * gain + bias


def inner_rows(left, right):
    return lax.dot_general(
        left, right, (((0,), (0,)), ((), ())), preferred_element_type=jnp.float32
    )


def times_transpose(left, right):
    return lax.dot_general(
        left, right, (((1,), (1,)), ((), ())), preferred_element_type=jnp.float32
    )


def allowed_rows(offset, number, seq_row, mask_table):
    group_tokens = seq_row.shape[0]
    table_width = mask_table.shape[1]
    query_pos = offset + jnp.arange(number, dtype=jnp.int32)
    key_pos = jnp.arange(group_tokens, dtype=jnp.int32)
    query_seq = lax.dynamic_slice_in_dim(seq_row, offset, number)
    table_rows = lax.dynamic_slice_in_dim(mask_table, offset // BLOCK, number // BLOCK, 0)
    spread = jnp.broadcast_to(
        table_rows[:, None, :, None], (number // BLOCK, BLOCK, table_width, BLOCK)
    ).reshape(number, group_tokens)
    return (
        (key_pos[None, :] <= query_pos[:, None])
        & (query_seq[:, None] == seq_row[None, :])
        & (spread == 1)
    )


def on_device(
    tokens,
    ln1_gain,
    ln1_bias,
    w_query,
    b_query,
    w_key,
    w_value,
    b_value,
    w_out,
    b_out,
    ln2_gain,
    ln2_bias,
    w_up,
    b_up,
    w_down,
    b_down,
    cotangent,
    seq_ids,
    block_mask,
    counts,
):
    row_count = tokens.shape[0]
    mp_size = lax.axis_size("mp")
    group_tokens = row_count * mp_size
    local_width = w_query.shape[1]
    local_heads = local_width // HD
    span = min(512, group_tokens)
    block_total = group_tokens // span
    scaling = HD ** (-0.5)
    seq_row = seq_ids[0]
    mask_table = block_mask[0]
    head_shape = (group_tokens, local_heads, HD)
    inputs = tokens.astype(jnp.float32)
    normed_float, pull_one = jax.vjp(layer_norm, inputs, ln1_gain, ln1_bias)
    normed_one = normed_float.astype(jnp.bfloat16)
    gathered_one = lax.all_gather(normed_one, "mp", axis=0, tiled=True)
    queries = (
        (jnp.dot(gathered_one, w_query, preferred_element_type=jnp.float32) + b_query)
        .astype(jnp.bfloat16)
        .reshape(head_shape)
    )
    key_rows = (
        jnp.dot(gathered_one, w_key, preferred_element_type=jnp.float32)
        .astype(jnp.bfloat16)
        .reshape(head_shape)
    )
    values = (
        (jnp.dot(gathered_one, w_value, preferred_element_type=jnp.float32) + b_value)
        .astype(jnp.bfloat16)
        .reshape(head_shape)
    )

    def forward_block(block_index):
        offset = block_index * span
        query_block = lax.dynamic_slice_in_dim(queries, offset, span, 0)
        scores = (
            jnp.einsum("qhd,khd->hqk", query_block, key_rows, preferred_element_type=jnp.float32)
            * scaling
        )
        allowed = allowed_rows(offset, span, seq_row, mask_table)
        scores = jnp.where(allowed[None], scores, -1e30)
        largest = jnp.max(scores, axis=-1, keepdims=True)
        exponent = jnp.exp(scores - largest)
        totals = jnp.sum(exponent, axis=-1, keepdims=True)
        weights = exponent / totals
        mixed = jnp.einsum(
            "hqk,khd->qhd", weights.astype(jnp.bfloat16), values, preferred_element_type=jnp.float32
        )
        return (
            mixed.reshape(span, local_width).astype(jnp.bfloat16),
            (largest + jnp.log(totals))[..., 0],
        )

    attended_blocks, log_totals = lax.map(forward_block, jnp.arange(block_total, dtype=jnp.int32))
    attended = attended_blocks.reshape(group_tokens, local_width)
    branch = lax.psum_scatter(
        jnp.dot(attended, w_out, preferred_element_type=jnp.float32),
        "mp",
        scatter_dimension=0,
        tiled=True,
    )
    middle = inputs + branch + b_out
    normed_mid, pull_two = jax.vjp(layer_norm, middle, ln2_gain, ln2_bias)
    normed_two = normed_mid.astype(jnp.bfloat16)
    gathered_two = lax.all_gather(normed_two, "mp", axis=0, tiled=True)
    hidden = jnp.dot(gathered_two, w_up, preferred_element_type=jnp.float32) + b_up
    activated_float, pull_gelu = jax.vjp(lambda point: jax.nn.gelu(point, approximate=True), hidden)
    activated = activated_float.astype(jnp.bfloat16)
    result = (
        middle
        + lax.psum_scatter(
            jnp.dot(activated, w_down, preferred_element_type=jnp.float32).astype(jnp.bfloat16),
            "mp",
            scatter_dimension=0,
            tiled=True,
        ).astype(jnp.float32)
        + b_down
    )
    group_index = lax.axis_index("dp")
    place = lax.axis_index("mp")
    dp_size = counts.shape[0]
    count_float = counts.astype(jnp.float32)
    is_here = jnp.arange(dp_size, dtype=jnp.int32) == group_index
    count_here = jnp.sum(jnp.where(is_here, counts, 0))
    weighting = dp_size * jnp.sum(jnp.where(is_here, count_float, 0.0)) / jnp.sum(count_float)
    positions = place * row_count + jnp.arange(row_count, dtype=jnp.int32)
    valid_rows = (positions < count_here).astype(jnp.float32)
    out_cot = cotangent.astype(jnp.float32) * valid_rows[:, None] * weighting
    grad_down_bias = jnp.sum(out_cot, axis=0)
    out_cot_low = out_cot.astype(jnp.bfloat16)
    gathered_cot = lax.all_gather(out_cot_low, "mp", axis=0, tiled=True)
    activated_cot = times_transpose(gathered_cot, w_down)
    grad_down = inner_rows(activated, gathered_cot)
    hidden_cot = pull_gelu(activated_cot)[0].astype(jnp.bfloat16)
    grad_up = inner_rows(gathered_two, hidden_cot)
    grad_up_bias = jnp.sum(hidden_cot, axis=0, dtype=jnp.float32)
    normed_two_cot = lax.psum_scatter(
        times_transpose(hidden_cot, w_up), "mp", scatter_dimension=0, tiled=True
    )
    middle_part, grad_gain_two, grad_bias_two = pull_two(normed_two_cot)
    middle_cot = out_cot + middle_part
    grad_out_bias = jnp.sum(middle_cot, axis=0)
    branch_cot = middle_cot.astype(jnp.bfloat16)
    gathered_branch = lax.all_gather(branch_cot, "mp", axis=0, tiled=True)
    attended_cot = times_transpose(gathered_branch, w_out).astype(jnp.bfloat16)
    grad_out = inner_rows(attended, gathered_branch)
    attended_cot = attended_cot.reshape(head_shape)

    def backward_block(carry, block_index):
        key_grad, value_grad = carry
        offset = block_index * span
        query_block = lax.dynamic_slice_in_dim(queries, offset, span, 0)
        cot_block = lax.dynamic_slice_in_dim(attended_cot, offset, span, 0)
        log_here = lax.dynamic_index_in_dim(log_totals, block_index, 0, keepdims=False)
        scores = (
            jnp.einsum("qhd,khd->hqk", query_block, key_rows, preferred_element_type=jnp.float32)
            * scaling
        )
        allowed = allowed_rows(offset, span, seq_row, mask_table)
        weights = jnp.where(allowed[None], jnp.exp(scores - log_here[..., None]), 0.0)
        weight_cot = jnp.einsum(
            "qhd,khd->hqk", cot_block, values, preferred_element_type=jnp.float32
        )
        centre = jnp.sum(weights * weight_cot, axis=-1, keepdims=True)
        score_cot = (weights * (weight_cot - centre)).astype(jnp.bfloat16)
        query_grad = (
            jnp.einsum("hqk,khd->qhd", score_cot, key_rows, preferred_element_type=jnp.float32)
            * scaling
        )
        key_grad = (
            key_grad
            + jnp.einsum("hqk,qhd->khd", score_cot, query_block, preferred_element_type=jnp.float32)
            * scaling
        )
        value_grad = value_grad + jnp.einsum(
            "hqk,qhd->khd",
            weights.astype(jnp.bfloat16),
            cot_block,
            preferred_element_type=jnp.float32,
        )
        return ((key_grad, value_grad), query_grad)

    zeros_start = jnp.zeros(head_shape, jnp.float32)
    (key_grad, value_grad), query_blocks = lax.scan(
        backward_block, (zeros_start, zeros_start), jnp.arange(block_total, dtype=jnp.int32)
    )
    query_low = query_blocks.reshape(group_tokens, local_width).astype(jnp.bfloat16)
    key_low = key_grad.reshape(group_tokens, local_width).astype(jnp.bfloat16)
    value_low = value_grad.reshape(group_tokens, local_width).astype(jnp.bfloat16)
    grad_query = inner_rows(gathered_one, query_low)
    grad_query_bias = jnp.sum(query_low, axis=0, dtype=jnp.float32)
    grad_key = inner_rows(gathered_one, key_low)
    grad_value = inner_rows(gathered_one, value_low)
    grad_value_bias = jnp.sum(value_low, axis=0, dtype=jnp.float32)
    normed_one_cot = lax.psum_scatter(
        times_transpose(query_low, w_query)
        + times_transpose(key_low, w_key)
        + times_transpose(value_low, w_value),
        "mp",
        scatter_dimension=0,
        tiled=True,
    )
    input_part, grad_gain_one, grad_bias_one = pull_one(normed_one_cot)
    grad_input = middle_cot + input_part
    small = lax.psum(
        (grad_gain_one, grad_bias_one, grad_out_bias, grad_gain_two, grad_bias_two, grad_down_bias),
        ("dp", "mp"),
    )
    large = lax.psum(
        (
            grad_query,
            grad_query_bias,
            grad_key,
            grad_value,
            grad_value_bias,
            grad_out,
            grad_up,
            grad_up_bias,
            grad_down,
        ),
        "dp",
    )
    return (
        result,
        grad_input,
        small[0],
        small[1],
        large[0],
        large[1],
        large[2],
        large[3],
        large[4],
        large[5],
        small[2],
        small[3],
        small[4],
        large[6],
        large[7],
        large[8],
        small[5],
    )


def solution(mesh):
    return jax.shard_map(
        on_device,
        mesh=mesh,
        in_specs=(
            P(("dp", "mp"), None),
            P(),
            P(),
            P(None, "mp"),
            P("mp"),
            P(None, "mp"),
            P(None, "mp"),
            P("mp"),
            P("mp", None),
            P(),
            P(),
            P(),
            P(None, "mp"),
            P("mp"),
            P("mp", None),
            P(),
            P(("dp", "mp"), None),
            P("dp", None),
            P("dp", None, None),
            P(),
        ),
        out_specs=(
            P(("dp", "mp"), None),
            P(("dp", "mp"), None),
            P(),
            P(),
            P(None, "mp"),
            P("mp"),
            P(None, "mp"),
            P(None, "mp"),
            P("mp"),
            P("mp", None),
            P(),
            P(),
            P(),
            P(None, "mp"),
            P("mp"),
            P("mp", None),
            P(),
        ),
        check_vma=False,
    )
```

profile of v0, /device:TPU:0, one launch (start us, length us, event | category | flops | bytes accessed | tf_op | source)
XLA Modules:
  0.0 1679.6 jit_solution(10199350876054711192)
XLA Ops:
  14.4 84.8 %all-gather.5.cloned.1.call-done = bf16[2048,2048]{1,0:T(8,128)(2,1)} async-done(((bf16[256,2048]{1,0:T(8,128)(2,1)}), bf16[2048,2048]{1,0:T(8,128)(2,1)}) %all-gather.5.cloned.1.call-update) | async-done | bytes 8388624 | tf_op jit(solution)/shard_map/all_gather | solution.py:85
  99.2 6.7 convolution_convert_fusion.2
  107.6 6.7 fusion.51
  116.0 7.0 fusion.52
  123.0 54.7 %while.31 = (s32[]{:T(128)}, bf16[4,512,256]{2,1,0:T(8,128)(2,1)}, f32[4,2,512]{2,1,0:T(2,128)S(1)}, s32[4]{0:T(128)S(1)}, s32[2048]{0:T(1024)S(1)}, /*index=5*/...) while((s32[]{:T(128)}, bf16[4,512,256]{2,1,0:T(8,128)(2,1)}, ...), condition=%wide.region_5.6_spmd, body=%wide.region_2.5_spmd.sunk | while | flops 1103232512 | bytes 41470496 | solution.py:123
  131.8 3.4 fusion.155
  145.4 3.4 fusion.155
  158.9 3.4 fusion.155
  172.5 3.4 fusion.155
  177.7 9.7 fusion.82
  187.5 166.7 %reduce-scatter.5.cloned.1.call-done = f32[256,2048]{1,0:T(8,128)} async-done(((f32[2048,2048]{1,0:T(8,128)}), f32[256,2048]{1,0:T(8,128)}) %reduce-scatter.5.cloned.1.call-update) | async-done | bytes 2097168 | tf_op jit(solution)/shard_map/reduce_scatter | solution.py:125
  363.7 76.0 %all-gather.7.cloned.1.call-done = bf16[2048,2048]{1,0:T(8,128)(2,1)} async-done(((bf16[256,2048]{1,0:T(8,128)(2,1)}), bf16[2048,2048]{1,0:T(8,128)(2,1)}) %all-gather.7.cloned.1.call-update) | async-done | bytes 8388624 | tf_op jit(solution)/shard_map/all_gather | solution.py:134
  439.6 14.6 fusion.83
  454.3 68.0 %all-gather.9.cloned.1.call-done = bf16[2048,2048]{1,0:T(8,128)(2,1)} async-done(((bf16[256,2048]{1,0:T(8,128)(2,1)}), bf16[2048,2048]{1,0:T(8,128)(2,1)}) %all-gather.9.cloned.1.call-update) | async-done | bytes 8388624 | tf_op jit(solution)/shard_map/all_gather | solution.py:160
  522.2 20.8 %convert_reduce_fusion = (f32[1024]{0:T(1024)}, bf16[2048,1024]{1,0:T(8,128)(2,1)S(1)}) fusion(f32[2048,1024]{1,0:T(8,128)} %fusion.83, f32[1024]{0:T(1024)S(1)} %copy-done.50, bf16[2048,2048]{1,0:T(8,128)(2,1)} %all-gather.9.cloned.1.call-done, bf16[1024,2048]{1,0:T(8,128)(2,1)} %param.38), kind=kOutput, calls=%fused_computation.62 | convolution fusion | flops 8638168064 | bytes 25174016 | tf_op jit(solution)/shard_map/dot_general | solution.py:27
  545.1 12.1 fusion.84
  557.3 15.4 convolution_convert_fusion
  572.8 151.2 %reduce-scatter.9.cloned.1.call-done = f32[256,2048]{1,0:T(8,128)} async-done(((f32[2048,2048]{1,0:T(8,128)}), f32[256,2048]{1,0:T(8,128)}) %reduce-scatter.9.cloned.1.call-update) | async-done | bytes 2097168 | tf_op jit(solution)/shard_map/reduce_scatter | solution.py:166
  724.0 3.5 multiply_reduce_fusion.1
  727.6 87.2 %reduce-scatter.7.cloned.1.call-done = bf16[256,2048]{1,0:T(8,128)(2,1)} async-done(((bf16[2048,2048]{1,0:T(8,128)(2,1)}), bf16[256,2048]{1,0:T(8,128)(2,1)}) %reduce-scatter.7.cloned.1.call-update) | async-done | bytes 1048592 | tf_op jit(solution)/shard_map/reduce_scatter | solution.py:140
  814.8 4.5 fusion.79
  824.2 78.5 %all-gather.11.cloned.1.call-done = bf16[2048,2048]{1,0:T(8,128)(2,1)} async-done(((bf16[256,2048]{1,0:T(8,128)(2,1)}), bf16[2048,2048]{1,0:T(8,128)(2,1)}) %all-gather.11.cloned.1.call-update) | async-done | bytes 8388624 | tf_op jit(solution)/shard_map/all_gather | solution.py:173
  902.8 6.7 convolution_convert_fusion.1
  909.5 88.9 %while.32 = (s32[]{:T(128)}, f32[2048,2,128]{0,2,1:T(8,128)}, f32[2048,2,128]{0,2,1:T(8,128)}, bf16[4,512,2,128]{3,1,2,0:T(8,128)(2,1)}, s32[4]{0:T(128)S(1)}, /...) while((s32[]{:T(128)}, f32[2048,2,128]{0,2,1:T(8,128)}, ...), condition=%wide.region_18.19_spmd.clone, body=%wide.region_16.18_spmd.clone.sunk | while | flops 2722758144 | bytes 118012680 | solution.py:213
  916.4 3.6 fusion.169
  920.0 4.0 multiply_reduce_fusion.5
  937.7 4.8 fusion.169
  942.5 4.0 multiply_reduce_fusion.5
  960.2 4.8 fusion.169
  964.9 4.0 multiply_reduce_fusion.5
  982.6 4.8 fusion.169
  987.4 4.0 multiply_reduce_fusion.5
  1004.3 8.2 fusion.85
  1012.6 8.1 fusion.65
  1020.7 18.4 %add_add_fusion = f32[2048,2048]{1,0:T(8,128)} fusion(f32[2048,2048]{1,0:T(8,128)} %fusion.65, f32[2048,2048]{1,0:T(8,128)} %fusion.85, bf16[2048,256]{0,1:T(8,128)(2,1)S(1)} %bitcast.145, bf16[2048,256]{1,0:T(8,128)(2,1)} %param.30), kind=kOutput, calls=%fused_computation.52 | convolution fusion | flops 2155872256 | bytes 52428800 | tf_op jit(solution)/shard_map/dot_general | solution.py:27
  1039.3 15.0 fusion.89
  1054.3 19.2 %fusion.76 = f32[1024,2048]{1,0:T(8,128)} fusion(bf16[2048,2048]{1,0:T(8,128)(2,1)} %all-gather.9.cloned.1.call-done, f32[2048,1024]{1,0:T(8,128)} %fusion.83, f32[1024]{0:T(1024)S(1)} %copy-done.51), kind=kOutput, calls=%fused_computation.125 | convolution fusion | flops 8610906112 | bytes 25169920 | tf_op jit(solution)/shard_map/dot_general | solution.py:21
  1073.5 7.2 fusion.88
  1080.7 3.9 fusion.87
  1084.6 3.8 fusion.86
  1088.4 3.8 fusion.63
  1093.8 11.0 all-reduce.1
  1104.7 101.3 %reduce-scatter.11.cloned.1.call-done = f32[256,2048]{1,0:T(8,128)} async-done(((f32[2048,2048]{1,0:T(8,128)}), f32[256,2048]{1,0:T(8,128)}) %reduce-scatter.11.cloned.1.call-update) | async-done | bytes 2097168 | tf_op jit(solution)/shard_map/reduce_scatter | solution.py:224
  1209.3 4.3 fusion.61
  1213.6 40.2 %all-reduce = (f32[2048]{0:T(1024)}, f32[2048]{0:T(1024)}, f32[2048]{0:T(1024)}, f32[2048]{0:T(1024)}, f32[2048]{0:T(1024)}, /*index=5*/f32[2048]{0:T(1024)}) all-reduce(f32[2048]{0:T(1024)S(1)} %get-tuple-element.403, f32[2048]{0:T(1024)S(1)} %get-tuple-element.406, ...), channel_id=1, replica_groups=mesh['dp'=4,'mp'=8] {'dp','mp'}, use_global_device_ids=true, to_apply=%region_23.24 | all-reduce | flops 12288 | bytes 98304 | tf_op jit(solution)/shard_map/psum | solution.py:234
  1253.8 400.9 %all-reduce.5.cloned.1.call-done = (f32[2048,256]{1,0:T(8,128)}, f32[2048,256]{1,0:T(8,128)}, f32[2048,256]{1,0:T(8,128)}, f32[256,2048]{1,0:T(8,128)}, f32[2048,1024]{1,0:T(8,128)}, /*index=5*/f32[1024,2048]{1,0:T(8,128)}) async-done(((f32[2048,256]{1,0:T(8,128)}, f32[2048,256]{1,0:T(8,128)}, f32[2048,256]{1,0:T(8,128)}, f32[256,2048]{1,0:T(8,128)}, f32[2048,1024]{1,0:T(8,128)}, ...) | async-done | bytes 25165840 | tf_op jit(solution)/shard_map/psum | solution.py:238
  1663.6 4.3 copy.111
  1669.2 3.4 copy.112
  (320 shorter events, 127.9 us)
Async XLA Ops:
  7.2 170.5 %copy-start = (bf16[256,2048]{1,0:T(8,128)(2,1)S(1)}, bf16[256,2048]{1,0:T(8,128)(2,1)}, u32[]{:S(2)}) copy-start(bf16[256,2048]{1,0:T(8,128)(2,1)} %param.32) | copy-start | bytes 3145732
  7.2 92.0 %copy-start.24 = (bf16[2048,256]{1,0:T(8,128)(2,1)S(1)}, bf16[2048,256]{1,0:T(8,128)(2,1)}, u32[]{:S(2)}) copy-start(bf16[2048,256]{1,0:T(8,128)(2,1)} %param.29) | copy-start | bytes 3145732
  7.2 92.0 %all-gather.5.cloned.1.call-start = ((), (), s32[]{:S(2)}) async-start(), calls=%async_computation.4 | async-start | bytes 9437184 | tf_op jit(solution)/shard_map/all_gather | solution.py:85
  14.3 339.9 %reduce-scatter.5.cloned.1.call-start = ((), (), s32[]{:S(2)}) async-start(), calls=%async_computation.5 | async-start | bytes 18874368 | tf_op jit(solution)/shard_map/reduce_scatter | solution.py:125
  14.4 93.2 %copy-start.26 = (bf16[2048,256]{1,0:T(8,128)(2,1)S(1)}, bf16[2048,256]{1,0:T(8,128)(2,1)}, u32[]{:S(2)}) copy-start(bf16[2048,256]{1,0:T(8,128)(2,1)} %param.27) | copy-start | bytes 3145732
  14.4 93.2 %copy-start.52 = (f32[256]{0:T(256)S(1)}, f32[256]{0:T(256)}, u32[]{:S(2)}) copy-start(f32[256]{0:T(256)} %param.28) | copy-start | bytes 3076
  107.6 8.4 copy-start.53
  116.0 7.0 copy-start.23
  116.0 7.0 copy-start.35
  177.7 9.7 copy-start.9
  187.4 166.8 %copy-start.5 = (bf16[256,2048]{1,0:T(8,128)(2,1)S(1)}, bf16[256,2048]{1,0:T(8,128)(2,1)}, u32[]{:S(2)}) copy-start(bf16[256,2048]{1,0:T(8,128)(2,1)} %param.24) | copy-start | bytes 3145732
  187.4 166.8 %copy-start.44 = (f32[2048]{0:T(1024)S(1)}, f32[2048]{0:T(1024)}, u32[]{:S(2)}) copy-start(f32[2048]{0:T(1024)} %param.33) | copy-start | bytes 24580
  187.5 170.1 %copy-start.30 = (f32[2048]{0:T(1024)S(1)}, f32[2048]{0:T(1024)}, u32[]{:S(2)}) copy-start(f32[2048]{0:T(1024)} %param.34) | copy-start | bytes 24580
  187.5 170.1 %copy-start.45 = (f32[2048]{0:T(1024)S(1)}, f32[2048]{0:T(1024)}, u32[]{:S(2)}) copy-start(f32[2048]{0:T(1024)} %param.35) | copy-start | bytes 24580
  187.5 252.2 %all-gather.7.cloned.1.call-start = ((), (), s32[]{:S(2)}) async-start(), calls=%async_computation.6 | async-start | bytes 9437184 | tf_op jit(solution)/shard_map/all_gather | solution.py:134
  356.2 6.1 copy-start.11
  359.0 163.2 %all-gather.9.cloned.1.call-start = ((), (), s32[]{:S(2)}) async-start(), calls=%async_computation.8 | async-start | bytes 9437184 | tf_op jit(solution)/shard_map/all_gather | solution.py:160
  362.3 457.0 %copy-start.38 = (f32[256]{0:T(256)}, f32[256]{0:T(256)S(1)}, u32[]{:S(2)}) copy-start(f32[256]{0:T(256)S(1)} %compare_convert_fusion) | copy-start | bytes 3076
  363.6 158.6 %copy-start.50 = (f32[1024]{0:T(1024)S(1)}, f32[1024]{0:T(1024)}, u32[]{:S(2)}) copy-start(f32[1024]{0:T(1024)} %param.37) | copy-start | bytes 12292
  363.6 360.4 %reduce-scatter.9.cloned.1.call-start = ((), (), s32[]{:S(2)}) async-start(), calls=%async_computation.9 | async-start | bytes 18874368 | tf_op jit(solution)/shard_map/reduce_scatter | solution.py:166
  522.2 22.9 %copy-start.49 = (bf16[2048,1024]{1,0:T(8,128)(2,1)S(1)}, bf16[2048,1024]{1,0:T(8,128)(2,1)}, u32[]{:S(2)}) copy-start(bf16[2048,1024]{1,0:T(8,128)(2,1)} %param.36) | copy-start | bytes 12582916
  557.2 257.5 %reduce-scatter.7.cloned.1.call-start = ((), (), s32[]{:S(2)}) async-start(), calls=%async_computation.7 | async-start | bytes 9437184 | tf_op jit(solution)/shard_map/reduce_scatter | solution.py:140
  572.7 242.0 %copy-start.46 = (f32[2048]{0:T(1024)S(1)}, f32[2048]{0:T(1024)}, u32[]{:S(2)}) copy-start(f32[2048]{0:T(1024)} %param.39) | copy-start | bytes 24580
  572.7 330.0 %all-gather.11.cloned.1.call-start = ((), (), s32[]{:S(2)}) async-start(), calls=%async_computation.10 | async-start | bytes 9437184 | tf_op jit(solution)/shard_map/all_gather | solution.py:173
  819.3 90.2 %copy-start.42 = (f32[256]{0:T(256)}, f32[256]{0:T(256)S(1)}, u32[]{:S(2)}) copy-start(f32[256]{0:T(256)S(1)} %negate_multiply_fusion.1) | copy-start | bytes 3076
  822.1 383.9 %reduce-scatter.11.cloned.1.call-start = ((), (), s32[]{:S(2)}) async-start(), calls=%async_computation.11 | async-start | bytes 18874368 | tf_op jit(solution)/shard_map/reduce_scatter | solution.py:224
  998.4 6.0 copy-start.25
  1004.3 16.4 copy-start.14
  1004.3 8.2 copy-start.27
  1039.2 15.1 copy-start.51
  1039.2 615.4 %all-reduce.5.cloned.1.call-start = ((), (), s32[]{:S(2)}) async-start(), calls=%async_computation.12 | async-start | bytes 50331648 | tf_op jit(solution)/shard_map/psum | solution.py:238
  1039.3 41.4 %slice-start.4 = ((s8[8388608]{0:T(1024)(128)(4,1)}), s8[4194304]{0:T(1024)(128)(4,1)S(1)}, s32[]{:S(2)}) async-start(s8[8388608]{0:T(1024)(128)(4,1)} %bitcast.162), calls=%async_computation.17 | async-start | bytes 8388608
  1054.3 19.2 %copy-start.13 = (bf16[4,512,256]{2,1,0:T(8,128)(2,1)S(1)}, bf16[4,512,256]{2,1,0:T(8,128)(2,1)}, u32[]{:S(2)}) copy-start(bf16[4,512,256]{2,1,0:T(8,128)(2,1)} %get-tuple-element.308) | copy-start | bytes 3145732
  1054.3 26.4 %slice-start.5 = ((s8[8388608]{0:T(1024)(128)(4,1)}), s8[4194304]{0:T(1024)(128)(4,1)S(1)}, s32[]{:S(2)}) async-start(s8[8388608]{0:T(1024)(128)(4,1)} %bitcast.162), calls=%async_computation.18 | async-start | bytes 8388608
  1073.5 7.2 copy-start.15
  1092.2 113.8 %copy-start.6 = (bf16[256,2048]{1,0:T(8,128)(2,1)S(1)}, bf16[256,2048]{1,0:T(8,128)(2,1)}, u32[]{:S(2)}) copy-start(bf16[256,2048]{1,0:T(8,128)(2,1)} %param.24) | copy-start | bytes 3145732
  1092.2 113.8 %copy-start.29 = (f32[2048]{0:T(1024)S(1)}, f32[2048]{0:T(1024)}, u32[]{:S(2)}) copy-start(f32[2048]{0:T(1024)} %param.25) | copy-start | bytes 24580
  1092.2 113.8 %copy-start.32 = (f32[256]{0:T(256)S(1)}, f32[256]{0:T(256)}, u32[]{:S(2)}) copy-start(f32[256]{0:T(256)} %copy-done.31) | copy-start | bytes 3076
  1093.4 114.8 %copy-start.41 = (f32[256]{0:T(256)S(1)}, f32[256]{0:T(256)}, u32[]{:S(2)}) copy-start(f32[256]{0:T(256)} %copy-done.40) | copy-start | bytes 3076
  1093.4 114.9 %copy-start.37 = (f32[256]{0:T(256)S(1)}, f32[256]{0:T(256)}, u32[]{:S(2)}) copy-start(f32[256]{0:T(256)} %copy-done.36) | copy-start | bytes 3076
  1093.4 115.8 %copy-start.12 = (bf16[256,2048]{1,0:T(8,128)(2,1)S(1)}, bf16[256,2048]{1,0:T(8,128)(2,1)}, u32[]{:S(2)}) copy-start(bf16[256,2048]{1,0:T(8,128)(2,1)} %param.40) | copy-start | bytes 3145732
  1093.4 115.8 %copy-start.39 = (f32[256]{0:T(256)S(1)}, f32[256]{0:T(256)}, u32[]{:S(2)}) copy-start(f32[256]{0:T(256)} %copy-done.38) | copy-start | bytes 3076
  1093.5 115.8 %copy-start.43 = (f32[256]{0:T(256)S(1)}, f32[256]{0:T(256)}, u32[]{:S(2)}) copy-start(f32[256]{0:T(256)} %copy-done.42) | copy-start | bytes 3076
  1654.6 4.5 copy-start.20
  1654.6 8.3 slice-start.2
  1659.2 4.4 slice-start.3
  1661.6 6.3 slice-start
  1663.6 5.6 slice-start.1
  (43 other events, 86.9 us)
Sparse Core Ops, SparseCore 0:
  14.4 84.7 all-gather.4
  187.6 166.6 reduce-scatter.4
  359.1 80.4 all-gather.6
  441.7 80.5 all-gather.8
  557.3 166.6 reduce-scatter.8
  726.8 87.9 reduce-scatter.6
  822.2 80.4 all-gather.10
  1039.3 166.6 reduce-scatter.10
  1211.7 442.8 all-reduce.4
where the time goes:
time: 1690 us; the launch traced here: 1680 us
  waiting for transfers between devices  1210 us (72%)
  matrix products  259 us (15%)
  other arithmetic  64.5 us (4%)
  local copies, waits for them, and re-layouts  59.1 us (3%)
  blocking collectives  51.2 us (3%)
    psum x1, waiting for transfers between devices, on_device(): lax.psum((grad_query, grad_query_bias, grad_key, grad_value, grad_value_b...  401 us
    reduce_scatter x1, waiting for transfers between devices, on_device(): lax.psum_scatter(jnp.dot(attended, w_out, preferred_element_type=jnp.floa...  167 us
    reduce_scatter x1, waiting for transfers between devices, on_device(): lax.psum_scatter(times_transpose(hidden_cot, w_up), 'mp', scatter_dimensi...  151 us
    reduce_scatter x1, waiting for transfers between devices, on_device(): lax.psum_scatter(times_transpose(query_low, w_query) + times_transpose(ke...  101 us
    reduce_scatter x1, waiting for transfers between devices, on_device(): lax.psum_scatter(jnp.dot(activated, w_down, preferred_element_type=jnp.fl...  87.2 us
    all_gather x1, waiting for transfers between devices, on_device(): gathered_one = lax.all_gather(normed_one, 'mp', axis=0, tiled=True)  84.8 us
    all_gather x1, waiting for transfers between devices, on_device(): gathered_branch = lax.all_gather(branch_cot, 'mp', axis=0, tiled=True)  78.5 us
    all_gather x1, waiting for transfers between devices, on_device(): gathered_two = lax.all_gather(normed_two, 'mp', axis=0, tiled=True)  76 us
  transfers between devices with their start and end apart: 9, of which 9 were waited for; matrix products, arithmetic and copies ran while one was open for 6% of the time, Pallas kernels for 0%

commit v1 on v0

v1 whole, which is shorter than its diff:
```python
import functools

import jax
import jax.numpy as jnp
from jax import lax
from jax.experimental import pallas as pl
from jax.experimental.pallas import tpu as pltpu
from jax.sharding import PartitionSpec as P

HD = 128
BLOCK = 256
SCALE = HD**-0.5
NEG = -1e30
epsilon = 1e-05
F32 = jnp.float32
BF16 = jnp.bfloat16


def norm_stats(values):
    average = jnp.mean(values, axis=-1, keepdims=True)
    centered = values - average
    variance = jnp.mean(centered * centered, axis=-1, keepdims=True)
    inverse = lax.rsqrt(variance + epsilon)
    return centered * inverse, inverse


def norm_back(normed, inverse, gain, cot):
    dn = cot * gain
    first = jnp.mean(dn, axis=-1, keepdims=True)
    second = jnp.mean(dn * normed, axis=-1, keepdims=True)
    return (dn - first - normed * second) * inverse


def dot(left, right):
    return jnp.dot(left, right, preferred_element_type=F32)


def inner_rows(left, right):
    return lax.dot_general(left, right, (((0,), (0,)), ((), ())), preferred_element_type=F32)


def times_transpose(left, right):
    return lax.dot_general(left, right, (((1,), (1,)), ((), ())), preferred_element_type=F32)


def attend_kernel(active, qkv, q_seq, k_seq, out, out_float, log_total, scores, top):
    blocks = pl.num_programs(1)
    here = pl.program_id(1)
    start = pl.multiple_of(here * BLOCK, BLOCK)
    query = qkv[pl.ds(start, BLOCK), :HD]
    row_seq = q_seq[...]
    rows = lax.broadcasted_iota(jnp.int32, (BLOCK, BLOCK), 0)
    cols = lax.broadcasted_iota(jnp.int32, (BLOCK, BLOCK), 1)
    top[...] = jnp.full((BLOCK, 1), NEG, F32)
    count = qkv.shape[0] // BLOCK
    for j in range(count):

        @pl.when(active[here * blocks + j] == 1)
        def _(j=j):
            part = times_transpose(query, qkv[j * BLOCK : (j + 1) * BLOCK, HD : 2 * HD])
            allow = (row_seq == k_seq[:, j * BLOCK : (j + 1) * BLOCK]) & (
                (cols <= rows) | (here != j)
            )
            part = jnp.where(allow, part * SCALE, NEG)
            scores[:, j * BLOCK : (j + 1) * BLOCK] = part
            top[...] = jnp.maximum(top[...], jnp.max(part, axis=-1, keepdims=True))

    biggest = top[...]
    out_float[...] = jnp.zeros((BLOCK, HD), F32)
    top[...] = jnp.zeros((BLOCK, 1), F32)
    for j in range(count):

        @pl.when(active[here * blocks + j] == 1)
        def _(j=j):
            part = jnp.exp(scores[:, j * BLOCK : (j + 1) * BLOCK] - biggest)
            top[...] += jnp.sum(part, axis=-1, keepdims=True)
            out_float[...] += dot(part.astype(BF16), qkv[j * BLOCK : (j + 1) * BLOCK, 2 * HD :])

    total = top[...]
    final = out_float[...] / total
    out_float[...] = final
    out[...] = final.astype(BF16)
    column = jnp.broadcast_to(biggest + jnp.log(total), (BLOCK, HD))
    log_total[0] = column.T[:8]


def attend(qkv, active, q_seq, k_seq):
    rows, width = qkv.shape
    heads = width // (3 * HD)
    blocks = rows // BLOCK
    grid_spec = pltpu.PrefetchScalarGridSpec(
        num_scalar_prefetch=1,
        grid=(heads, blocks),
        in_specs=[
            pl.BlockSpec((rows, 3 * HD), lambda h, i, a: (0, h)),
            pl.BlockSpec((BLOCK, 1), lambda h, i, a: (i, 0)),
            pl.BlockSpec((1, rows), lambda h, i, a: (0, 0)),
        ],
        out_specs=[
            pl.BlockSpec((BLOCK, HD), lambda h, i, a: (i, h)),
            pl.BlockSpec((BLOCK, HD), lambda h, i, a: (i, h)),
            pl.BlockSpec((1, 8, BLOCK), lambda h, i, a: (h, 0, i)),
        ],
        scratch_shapes=[pltpu.VMEM((BLOCK, rows), F32), pltpu.VMEM((BLOCK, 1), F32)],
    )
    return pl.pallas_call(
        attend_kernel,
        grid_spec=grid_spec,
        out_shape=[
            jax.ShapeDtypeStruct((rows, heads * HD), BF16),
            jax.ShapeDtypeStruct((rows, heads * HD), F32),
            jax.ShapeDtypeStruct((heads, 8, rows), F32),
        ],
        cost_estimate=pl.CostEstimate(
            flops=2 * heads * rows * rows * HD,
            bytes_accessed=rows * width * 4,
            transcendentals=heads * rows * rows // 2,
        ),
        name="attend",
    )(active, qkv, q_seq, k_seq)


def attend_back_kernel(
    active, qkv, cot, out_float, log_total, k_seq_col, q_seq_row, grad, key_acc, value_acc, query_acc
):
    blocks = pl.num_programs(1)
    here = pl.program_id(1)
    count = qkv.shape[0] // BLOCK
    start = pl.multiple_of(here * BLOCK, BLOCK)

    @pl.when(here == 0)
    def _():
        key_acc[...] = jnp.zeros(key_acc.shape, F32)
        value_acc[...] = jnp.zeros(value_acc.shape, F32)

    query = qkv[pl.ds(start, BLOCK), :HD]
    cot_here = cot[...]
    centre = jnp.sum(cot_here.astype(F32) * out_float[...], axis=-1, keepdims=True)
    centre = jnp.broadcast_to(centre, (BLOCK, HD)).T[:1]
    log_row = log_total[0, :1]
    row_seq = q_seq_row[...]
    keys = lax.broadcasted_iota(jnp.int32, (BLOCK, BLOCK), 0)
    queries = lax.broadcasted_iota(jnp.int32, (BLOCK, BLOCK), 1)
    query_acc[...] = jnp.zeros((BLOCK, HD), F32)
    for j in range(count):

        @pl.when(active[here * blocks + j] == 1)
        def _(j=j):
            spot = slice(j * BLOCK, (j + 1) * BLOCK)
            key = qkv[spot, HD : 2 * HD]
            part = times_transpose(key, query)
            allow = (k_seq_col[spot, :] == row_seq) & ((keys <= queries) | (here != j))
            weight = jnp.where(allow, jnp.exp(part * SCALE - log_row), 0.0)
            weight_cot = times_transpose(qkv[spot, 2 * HD :], cot_here)
            score_cot = (weight * (weight_cot - centre)).astype(BF16)
            value_acc[spot, :] += dot(weight.astype(BF16), cot_here)
            key_acc[spot, :] += dot(score_cot, query)
            query_acc[...] += inner_rows(score_cot, key)

    grad[pl.ds(start, BLOCK), :HD] = (query_acc[...] * SCALE).astype(BF16)

    @pl.when(here == blocks - 1)
    def _():
        grad[:, HD : 2 * HD] = (key_acc[...] * SCALE).astype(BF16)
        grad[:, 2 * HD :] = value_acc[...].astype(BF16)


def attend_back(qkv, cot, out_float, log_total, active, k_seq_col, q_seq_row):
    rows, width = qkv.shape
    heads = width // (3 * HD)
    blocks = rows // BLOCK
    grid_spec = pltpu.PrefetchScalarGridSpec(
        num_scalar_prefetch=1,
        grid=(heads, blocks),
        in_specs=[
            pl.BlockSpec((rows, 3 * HD), lambda h, i, a: (0, h)),
            pl.BlockSpec((BLOCK, HD), lambda h, i, a: (i, h)),
            pl.BlockSpec((BLOCK, HD), lambda h, i, a: (i, h)),
            pl.BlockSpec((1, 8, BLOCK), lambda h, i, a: (h, 0, i)),
            pl.BlockSpec((rows, 1), lambda h, i, a: (0, 0)),
            pl.BlockSpec((1, BLOCK), lambda h, i, a: (0, i)),
        ],
        out_specs=pl.BlockSpec((rows, 3 * HD), lambda h, i, a: (0, h)),
        scratch_shapes=[
            pltpu.VMEM((rows, HD), F32),
            pltpu.VMEM((rows, HD), F32),
            pltpu.VMEM((BLOCK, HD), F32),
        ],
    )
    return pl.pallas_call(
        attend_back_kernel,
        grid_spec=grid_spec,
        out_shape=jax.ShapeDtypeStruct((rows, width), BF16),
        cost_estimate=pl.CostEstimate(
            flops=5 * heads * rows * rows * HD,
            bytes_accessed=rows * width * 6,
            transcendentals=heads * rows * rows // 2,
        ),
        name="attend_back",
    )(active, qkv, cot, out_float, log_total, k_seq_col, q_seq_row)


class Line:
    def __init__(self):
        self.length = lax.axis_size("mp") // 2
        place = lax.axis_index("mp")
        self.chip = place // 2
        self.core = place % 2
        size = self.length
        self.order = []
        for z in range(size):
            side = 1 if z < size // 2 else -1
            others = [d for d in range(-z, size - z) if d != 0]
            others.sort(key=lambda d: (abs(d), -d * side))
            self.order.append([z] + [z + d for d in others])

    def chips(self):
        return jnp.asarray(self.order, jnp.int32)[self.chip]

    def pairs(self, links):
        return [(2 * a + c, 2 * b + c) for a, b in links for c in range(2)]

    def move(self, value, links):
        return lax.ppermute(value, "mp", self.pairs(links))

    def swap(self, value):
        return lax.ppermute(value, "mp", [(m, m ^ 1) for m in range(2 * self.length)])

    def choose(self, by_chip):
        groups = []
        for z, value in enumerate(by_chip):
            if value is None:
                continue
            for entry in groups:
                if entry[0] is value:
                    entry[1].append(z)
                    break
            else:
                groups.append((value, [z]))
        result = groups[0][0]
        for value, where in groups[1:]:
            hit = functools.reduce(jnp.logical_or, [self.chip == z for z in where])
            result = jnp.where(hit, value, result)
        return result

    def pair(self, mine):
        other = self.swap(mine)
        first = self.core == 0
        return jnp.concatenate(
            [jnp.where(first, mine, other), jnp.where(first, other, mine)], axis=0
        )

    def gather(self, mine):
        size = self.length
        right, left = [mine], [mine]
        slots = [self.pair(mine)]
        for k in range(1, size):
            if k == size - 1 and size > 2:
                value = jnp.where(self.chip < size // 2, left[-1], right[-1])
                got = self.move(value, [(size - 2, size - 1), (1, 0)])
                right.append(got)
                left.append(got)
            else:
                right.append(self.move(right[-1], [(i, i + 1) for i in range(k - 1, size - 1)]))
                left.append(self.move(left[-1], [(i, i - 1) for i in range(1, size - k + 1)]))
            source = []
            for z in range(size):
                d = self.order[z][k] - z
                source.append(left[d] if d > 0 else right[-d])
            slots.append(self.pair(self.choose(source)))
        return slots

    def scatter(self, parts):
        size = self.length
        rows = parts[0].shape[0] // 2
        first = self.core == 0
        sums = []
        for part in parts:
            low, high = part[:rows], part[rows:]
            other = self.swap(jnp.where(first, high, low))
            sums.append(
                (jnp.where(first, low, high).astype(F32) + other.astype(F32)).astype(BF16)
            )
        spot = [{chip: k for k, chip in enumerate(row)} for row in self.order]
        from_left = from_right = None
        for k in range(size - 1, 0, -1):
            go_right = [
                sums[spot[z][z + k]] if z + k < size else None for z in range(size)
            ]
            go_left = [sums[spot[z][z - k]] if z >= k else None for z in range(size)]
            if 2 * k > size - 1:
                both = [r if r is not None else m for r, m in zip(go_right, go_left)]
                value = self.choose(both)
                if from_left is not None:
                    came = from_left
                    if from_right is not from_left:
                        came = jnp.where(self.chip < size // 2, from_left, from_right)
                    value = (value.astype(F32) + came.astype(F32)).astype(BF16)
                send_right = send_left = value
            else:
                send_right = (self.choose(go_right).astype(F32) + from_left.astype(F32)).astype(BF16)
                send_left = (self.choose(go_left).astype(F32) + from_right.astype(F32)).astype(BF16)
            to_right = [(i, i + 1) for i in range(size - k)]
            to_left = [(i, i - 1) for i in range(k, size)]
            if k == size - 1 and size > 2:
                from_left = from_right = self.move(send_right, to_right + to_left)
            else:
                from_left = self.move(send_right, to_right)
                from_right = self.move(send_left, to_left)
        return sums[0].astype(F32) + from_left.astype(F32) + from_right.astype(F32)


def sum_over_dp(value):
    size = lax.axis_size("dp")
    index = lax.axis_index("dp")
    bits = size.bit_length() - 1
    half = value.shape[0] // 2
    pieces = []
    for piece, order in (
        (value[:half], list(range(bits))),
        (value[half:], list(range(bits))[::-1]),
    ):
        for b in order:
            links = [(i, i ^ (1 << b)) for i in range(size)]
            mid = piece.shape[0] // 2
            low_side = ((index >> b) & 1) == 0
            keep = jnp.where(low_side, piece[:mid], piece[mid:])
            send = jnp.where(low_side, piece[mid:], piece[:mid])
            came = lax.ppermute(send, "dp", links)
            piece = (keep.astype(F32) + came.astype(F32)).astype(BF16)
        for b in order[::-1]:
            links = [(i, i ^ (1 << b)) for i in range(size)]
            low_side = ((index >> b) & 1) == 0
            came = lax.ppermute(piece, "dp", links)
            piece = jnp.concatenate(
                [jnp.where(low_side, piece, came), jnp.where(low_side, came, piece)], axis=0
            )
        pieces.append(piece)
    return jnp.concatenate(pieces, axis=0).astype(F32)


def after(value, *others):
    return lax.optimization_barrier((value, *others))[0]


ROOT = 0.7978845608028654
CUBE = 0.044715


def gelu_and_slope(point):
    inside = jnp.tanh(ROOT * (point + CUBE * point * point * point))
    value = 0.5 * point * (1.0 + inside)
    slope = 0.5 * (1.0 + inside) + 0.5 * point * (1.0 - inside * inside) * ROOT * (
        1.0 + 3.0 * CUBE * point * point
    )
    return value, slope


def on_device(
    tokens,
    ln1_gain,
    ln1_bias,
    w_query,
    b_query,
    w_key,
    w_value,
    b_value,
    w_out,
    b_out,
    ln2_gain,
    ln2_bias,
    w_up,
    b_up,
    w_down,
    b_down,
    cotangent,
    seq_ids,
    block_mask,
    counts,
):
    rows = tokens.shape[0]
    line = Line()
    size = line.length
    both = 2 * rows
    group = both * size
    width = w_query.shape[1]
    heads = width // HD
    mp_size = lax.axis_size("mp")
    place = lax.axis_index("mp")
    chips = line.chips()

    cut = [slice(h * HD, (h + 1) * HD) for h in range(heads)]
    w_qkv = jnp.concatenate([w[:, s] for s in cut for w in (w_query, w_key, w_value)], axis=1)
    nothing = jnp.zeros_like(b_query)
    b_qkv = jnp.concatenate([b[s] for s in cut for b in (b_query, nothing, b_value)])

    blocks = group // BLOCK
    per_chip = both // BLOCK
    seq_slots = seq_ids[0].reshape(size, both)[chips]
    seq_flat = seq_slots.reshape(group)
    block_ids = (chips[:, None] * per_chip + jnp.arange(per_chip, dtype=jnp.int32)).reshape(blocks)
    in_blocks = seq_flat.reshape(blocks, BLOCK)
    low, high = jnp.min(in_blocks, axis=1), jnp.max(in_blocks, axis=1)
    mask = block_mask[0][block_ids][:, block_ids]
    active = (
        (mask == 1)
        & (block_ids[None, :] <= block_ids[:, None])
        & (low[None, :] <= high[:, None])
        & (low[:, None] <= high[None, :])
    )
    active = active.astype(jnp.int32).reshape(blocks * blocks)
    seq_column, seq_row = seq_flat[:, None], seq_flat[None, :]

    dp_size = counts.shape[0]
    count_float = counts.astype(F32)
    is_here = jnp.arange(dp_size, dtype=jnp.int32) == lax.axis_index("dp")
    count_here = jnp.sum(jnp.where(is_here, counts, 0))
    weighting = dp_size * jnp.sum(jnp.where(is_here, count_float, 0.0)) / jnp.sum(count_float)
    positions = place * rows + jnp.arange(rows, dtype=jnp.int32)
    valid_rows = (positions < count_here).astype(F32)
    out_cot = cotangent.astype(F32) * valid_rows[:, None] * weighting
    grad_down_bias = jnp.sum(out_cot, axis=0)

    inputs = tokens.astype(F32)
    normed_one, inverse_one = norm_stats(inputs)
    first = (normed_one * ln1_gain + ln1_bias).astype(BF16)
    slots_one = line.gather(first)
    qkv = jnp.concatenate(
        [(dot(slot, w_qkv) + b_qkv).astype(BF16) for slot in slots_one], axis=0
    )
    out_low = after(out_cot.astype(BF16), slots_one[-1])
    gathered_cot = lax.all_gather(out_low, "mp", axis=0, tiled=True)
    attended, attended_float, log_total = attend(qkv, active, seq_column, seq_row)
    branch = line.scatter(
        [dot(attended[k * both : (k + 1) * both], w_out).astype(BF16) for k in range(size)]
    )
    activated_cot = times_transpose(gathered_cot, w_down)
    middle = inputs + branch + b_out
    normed_two, inverse_two = norm_stats(middle)
    second = (normed_two * ln2_gain + ln2_bias).astype(BF16)
    slots_two = line.gather(second)

    activated_slots, hidden_cots, parts_two = [], [], []
    for k in range(size):
        hidden = dot(slots_two[k], w_up) + b_up
        value, slope = gelu_and_slope(hidden)
        cot_here = lax.dynamic_slice_in_dim(activated_cot, chips[k] * both, both, 0)
        activated_slots.append(value.astype(BF16))
        hidden_cots.append((cot_here * slope).astype(BF16))
        parts_two.append(times_transpose(hidden_cots[k], w_up).astype(BF16))
    normed_two_cot = line.scatter(parts_two)
    activated = jnp.zeros((group, w_up.shape[1]), BF16)
    for k in range(size):
        activated = lax.dynamic_update_slice_in_dim(
            activated, activated_slots[k], chips[k] * both, 0
        )
    last = lax.psum_scatter(
        dot(activated, w_down).astype(BF16), "mp", scatter_dimension=0, tiled=True
    )
    result = middle + last.astype(F32) + b_down
    hidden_cot = jnp.concatenate(hidden_cots, axis=0)
    grad_down = inner_rows(activated, gathered_cot).astype(BF16)
    grad_up = inner_rows(jnp.concatenate(slots_two, axis=0), hidden_cot).astype(BF16)
    grad_up_bias = jnp.sum(hidden_cot, axis=0, dtype=F32)

    grad_gain_two = jnp.sum(normed_two_cot * normed_two, axis=0)
    grad_bias_two = jnp.sum(normed_two_cot, axis=0)
    middle_cot = out_cot + norm_back(normed_two, inverse_two, ln2_gain, normed_two_cot)
    grad_out_bias = jnp.sum(middle_cot, axis=0)
    slots_three = line.gather(middle_cot.astype(BF16))
    attended_cot = jnp.concatenate(
        [times_transpose(slot, w_out).astype(BF16) for slot in slots_three], axis=0
    )
    grad_out = inner_rows(attended, jnp.concatenate(slots_three, axis=0)).astype(BF16)

    cot_qkv = attend_back(
        qkv, attended_cot, attended_float, log_total, active, seq_column, seq_row
    )
    normed_one_cot = line.scatter(
        [
            times_transpose(cot_qkv[k * both : (k + 1) * both], w_qkv).astype(BF16)
            for k in range(size)
        ]
    )
    grad_qkv = inner_rows(jnp.concatenate(slots_one, axis=0), cot_qkv).astype(BF16)
    grad_qkv_bias = jnp.sum(cot_qkv, axis=0, dtype=F32)
    grad_input = middle_cot + norm_back(normed_one, inverse_one, ln1_gain, normed_one_cot)
    grad_gain_one = jnp.sum(normed_one_cot * normed_one, axis=0)
    grad_bias_one = jnp.sum(normed_one_cot, axis=0)

    sum_down = sum_over_dp(grad_down)
    sum_up = sum_over_dp(grad_up)
    sum_out = sum_over_dp(grad_out)
    sum_qkv = sum_over_dp(grad_qkv)

    biases = jnp.concatenate([grad_qkv_bias, grad_up_bias])
    spread = jnp.where(
        jnp.arange(mp_size, dtype=jnp.int32)[:, None] == place, biases[None, :], 0.0
    )
    small, spread = lax.psum(
        (
            jnp.stack(
                [
                    grad_gain_one,
                    grad_bias_one,
                    grad_out_bias,
                    grad_gain_two,
                    grad_bias_two,
                    grad_down_bias,
                ]
            ),
            spread,
        ),
        ("dp", "mp"),
    )
    biases = lax.dynamic_index_in_dim(spread, place, 0, keepdims=False)

    def columns(array, which):
        return jnp.concatenate(
            [
                array[..., (3 * h + which) * HD : (3 * h + which + 1) * HD]
                for h in range(heads)
            ],
            axis=-1,
        )

    return (
        result,
        grad_input,
        small[0],
        small[1],
        columns(sum_qkv, 0),
        columns(biases[: 3 * width], 0),
        columns(sum_qkv, 1),
        columns(sum_qkv, 2),
        columns(biases[: 3 * width], 2),
        sum_out,
        small[2],
        small[3],
        small[4],
        sum_up,
        biases[3 * width :],
        sum_down,
        small[5],
    )


def solution(mesh):
    rows = P(("dp", "mp"), None)
    wide = P(None, "mp")
    tall = P("mp", None)
    return jax.shard_map(
        on_device,
        mesh=mesh,
        in_specs=(
            rows,
            P(),
            P(),
            wide,
            P("mp"),
            wide,
            wide,
            P("mp"),
            tall,
            P(),
            P(),
            P(),
            wide,
            P("mp"),
            tall,
            P(),
            rows,
            P("dp", None),
            P("dp", None, None),
            P(),
        ),
        out_specs=(
            rows,
            rows,
            P(),
            P(),
            wide,
            P("mp"),
            wide,
            wide,
            P("mp"),
            tall,
            P(),
            P(),
            P(),
            wide,
            P("mp"),
            tall,
            P(),
        ),
        check_vma=False,
    )
```

time: 1690 us -> 1110 us (0.66)
  waiting for transfers between devices: 1210 us -> 590 us
  starting transfers between devices: 0.37 us -> 157 us
  matrix products: 259 us -> 121 us
  other arithmetic: 64.5 us -> 128 us
  Pallas kernels: 0 us -> 60.1 us
  blocking collectives: 51.2 us -> 0 us
  local copies, waits for them, and re-layouts: 59.1 us -> 32.9 us
    reduce_scatter x4 -> x1, waiting for transfers between devices: 506 us -> 0.01 us  [on_device(): lax.psum_scatter(dot(activated, w_down).astype(BF16), 'mp', scatter_dimen...]
    ppermute x0 -> x86, waiting for transfers between devices: none -> 470 us  [the longest x30 327 us: move(): return lax.ppermute(value, 'mp', self.pairs(links))]
    all_gather x4 -> x1, waiting for transfers between devices: 307 us -> 0.01 us  [on_device(): gathered_cot = lax.all_gather(out_low, 'mp', axis=0, tiled=True)]
    psum x1, waiting for transfers between devices: 401 us -> 119 us  [on_device(): lax.psum((jnp.stack([grad_gain_one, grad_bias_one, grad_out_bias, grad_ga...]
    ppermute x0 -> x86, starting transfers between devices: none -> 157 us  [the longest x30 119 us: move(): return lax.ppermute(value, 'mp', self.pairs(links))]
    dot_general x34 -> x13, matrix products: 132 us -> 46.2 us  [dot(): return jnp.dot(left, right, preferred_element_type=F32)]
    pallas_call x0 -> x2, Pallas kernels: none -> 60.1 us  [the longest x1 30.3 us: attend_back(): pl.pallas_call(attend_back_kernel, grid_spec=grid_spec, out_shape=jax.Sha...]
    psum x2 -> x0, blocking collectives: 51.2 us -> none  [the longest x1 40.2 us: on_device(): lax.psum((grad_gain_one, grad_bias_one, grad_out_bias, grad_gain_two, gra...]
  transfers between devices with their start and end apart: 9 -> 89, of which waited for: 9 -> 41; matrix products, arithmetic and copies ran while one was open for 6% -> 16% of each run, Pallas kernels for 0% -> 0%
where the time goes in v1:
time: 1110 us
  waiting for transfers between devices  590 us (53%)
  starting transfers between devices  157 us (14%)
  other arithmetic  128 us (12%)
  matrix products  121 us (11%)
  Pallas kernels  60.1 us (5%)
  local copies, waits for them, and re-layouts  32.9 us (3%)
  between operations  20.3 us (2%)
    ppermute x30, waiting for transfers between devices, move(): return lax.ppermute(value, 'mp', self.pairs(links))  327 us
    psum x1, waiting for transfers between devices, on_device(): lax.psum((jnp.stack([grad_gain_one, grad_bias_one, grad_out_bias, grad_ga...  119 us
    ppermute x30, starting transfers between devices, move(): return lax.ppermute(value, 'mp', self.pairs(links))  119 us
    ppermute x16, waiting for transfers between devices, sum_over_dp(): came = lax.ppermute(send, 'dp', links)  76.8 us
    ppermute x16, waiting for transfers between devices, sum_over_dp(): came = lax.ppermute(piece, 'dp', links)  59.3 us
    dot_general x13, matrix products, dot(): return jnp.dot(left, right, preferred_element_type=F32)  46.2 us
    dot_general x4, matrix products, inner_rows(): lax.dot_general(left, right, (((0,), (0,)), ((), ())), preferred_element_...  37.7 us
    dot_general x13, matrix products, times_transpose(): lax.dot_general(left, right, (((1,), (1,)), ((), ())), preferred_element_...  36.7 us
  transfers between devices with their start and end apart: 89, of which 41 were waited for; matrix products, arithmetic and copies ran while one was open for 16% of the time, Pallas kernels for 0%

profile of v1, /device:TPU:0, one launch (start us, length us, event | category | flops | bytes accessed | tf_op | source)
XLA Modules:
  0.0 1108.3 jit_solution(13876410395481073947)
XLA Ops:
  13.4 6.6 collective-permute-start.1
  28.3 12.2 %collective-permute-done.2 = bf16[256,2048]{1,0:T(8,128)(2,1)} collective-permute-done((bf16[256,2048]{1,0:T(8,128)(2,1)}, bf16[256,2048]{1,0:T(8,128)(2,1)}, u32[]{:S(2)}, u32[]{:S(2)}) %collective-permute-start.2) | collective-permute-done | bytes 1048608 | tf_op jit(solution)/shard_map/ppermute | solution.py:224
  45.4 21.5 %collective-permute-done.5 = bf16[256,2048]{1,0:T(8,128)(2,1)S(1)} collective-permute-done((bf16[256,2048]{1,0:T(8,128)(2,1)}, bf16[256,2048]{1,0:T(8,128)(2,1)S(1)}, u32[]{:S(2)}, u32[]{:S(2)}) %collective-permute-start.5) | collective-permute-done | bytes 1048608 | tf_op jit(solution)/shard_map/ppermute | solution.py:224
  75.1 19.5 %collective-permute-done.7 = bf16[256,2048]{1,0:T(8,128)(2,1)} collective-permute-done((bf16[256,2048]{1,0:T(8,128)(2,1)}, bf16[256,2048]{1,0:T(8,128)(2,1)}, u32[]{:S(2)}, u32[]{:S(2)}) %collective-permute-start.7) | collective-permute-done | bytes 1048608 | tf_op jit(solution)/shard_map/ppermute | solution.py:224
  115.7 29.8 %attend.1 = (bf16[2048,256]{1,0:T(8,128)(2,1)}, f32[2048,256]{1,0:T(8,128)}, f32[2,8,2048]{2,1,0:T(8,128)}) custom-call(s32[64]{0:T(128)} %reshape.227.active, bf16[2048,768]{1,0:T(8,128)(2,1)} %pad_maximum_fusion.1.qkv, s32[2048,1]{1,0:T(8,128)} %bitcast.88, s32[1,2048]{1,0:T(1,128)} %bitcast.99), custom_call_target="tpu_custom_call" | custom-call | flops 2147483648 | bytes 6291456 | tf_op jit(solution)/shard_map/attend/pallas_call | solution.py:106
  164.0 16.1 %collective-permute-done.13 = bf16[256,2048]{1,0:T(8,128)(2,1)} collective-permute-done((bf16[256,2048]{1,0:T(8,128)(2,1)}, bf16[256,2048]{1,0:T(8,128)(2,1)}, u32[]{:S(2)}, u32[]{:S(2)}) %collective-permute-start.13) | collective-permute-done | bytes 1048608 | tf_op jit(solution)/shard_map/ppermute | solution.py:224
  184.1 5.7 collective-permute-start.14
  193.8 28.7 %collective-permute-done.14 = bf16[256,2048]{1,0:T(8,128)(2,1)} collective-permute-done((bf16[256,2048]{1,0:T(8,128)(2,1)}, bf16[256,2048]{1,0:T(8,128)(2,1)}, u32[]{:S(2)}, u32[]{:S(2)}) %collective-permute-start.14) | collective-permute-done | bytes 1048608 | tf_op jit(solution)/shard_map/ppermute | solution.py:224
  225.2 26.4 %collective-permute-start.15 = (bf16[256,2048]{1,0:T(8,128)(2,1)S(1)}, bf16[256,2048]{1,0:T(8,128)(2,1)S(1)}, u32[]{:S(2)}, u32[]{:S(2)}) collective-permute-start(bf16[256,2048]{1,0:T(8,128)(2,1)S(1)} %get-tuple-element.101), channel_id=1, source_target_pairs={{0,2},{1,3},{2,4},{3,5},{4,6},{5,7},{8,10},{9,11},{10,12},{11,13},... | collective-permute-start | bytes 3145736 | tf_op jit(solution)/shard_map/ppermute | solution.py:224
  253.8 41.0 %collective-permute-done.15 = bf16[256,2048]{1,0:T(8,128)(2,1)S(1)} collective-permute-done((bf16[256,2048]{1,0:T(8,128)(2,1)S(1)}, bf16[256,2048]{1,0:T(8,128)(2,1)S(1)}, u32[]{:S(2)}, u32[]{:S(2)}) %collective-permute-start.15) | collective-permute-done | bytes 1048608 | tf_op jit(solution)/shard_map/ppermute | solution.py:224
  294.8 7.7 collective-permute-done.17
  307.1 13.1 %collective-permute-start.19 = (bf16[256,2048]{1,0:T(8,128)(2,1)}, bf16[256,2048]{1,0:T(8,128)(2,1)S(1)}, u32[]{:S(2)}, u32[]{:S(2)}) collective-permute-start(bf16[256,2048]{1,0:T(8,128)(2,1)} %add_convert_fusion.18), channel_id=1, source_target_pairs={{0,2},{1,3},{2,4},{3,5},{4,6},{5,7},{8,10},{9,11},{10,12},{11,13},... | collective-permute-start | bytes 3145736 | tf_op jit(solution)/shard_map/ppermute | solution.py:224
  320.2 19.8 %collective-permute-done.20 = bf16[256,2048]{1,0:T(8,128)(2,1)S(1)} collective-permute-done((bf16[256,2048]{1,0:T(8,128)(2,1)}, bf16[256,2048]{1,0:T(8,128)(2,1)S(1)}, u32[]{:S(2)}, u32[]{:S(2)}) %collective-permute-start.20) | collective-permute-done | bytes 1048608 | tf_op jit(solution)/shard_map/ppermute | solution.py:224
  342.0 22.6 %collective-permute-done.23 = bf16[256,2048]{1,0:T(8,128)(2,1)S(1)} collective-permute-done((bf16[256,2048]{1,0:T(8,128)(2,1)S(1)}, bf16[256,2048]{1,0:T(8,128)(2,1)S(1)}, u32[]{:S(2)}, u32[]{:S(2)}) %collective-permute-start.23) | collective-permute-done | bytes 1048608 | tf_op jit(solution)/shard_map/ppermute | solution.py:224
  372.1 18.9 %collective-permute-done.25 = bf16[256,2048]{1,0:T(8,128)(2,1)} collective-permute-done((bf16[256,2048]{1,0:T(8,128)(2,1)}, bf16[256,2048]{1,0:T(8,128)(2,1)}, u32[]{:S(2)}, u32[]{:S(2)}) %collective-permute-start.25) | collective-permute-done | bytes 1048608 | tf_op jit(solution)/shard_map/ppermute | solution.py:224
  417.5 14.9 %fusion.146 = f32[2048,1024]{1,0:T(8,128)} fusion(bf16[2048,2048]{1,0:T(8,128)(2,1)} %all-gather.2.cloned.1.call-done, bf16[1024,2048]{1,0:T(8,128)(2,1)} %param.35), kind=kOutput, calls=%fused_computation.401 | convolution fusion | flops 8589934592 | bytes 20971520 | tf_op jit(solution)/shard_map/dot_general | solution.py:43
  432.4 11.3 %fusion.27 = (bf16[512,1024]{1,0:T(8,128)(2,1)S(1)}, bf16[512,1024]{1,0:T(8,128)(2,1)S(1)}, bf16[512,1024]{1,0:T(8,128)(2,1)S(1)}, bf16[512,1024]{1,0:T(8,128)(2,1)}, f32[512,1024]{1,0:T(8,128)S(1)}) fusion(f32[2048,1024]{1,0:T(8,128)} %fusion.146, s32[]{:T(128)S(6)} %select_n.737, f32[1024]{0:T(1024)S(1)} %copy-done.56, f32[512,1024]{1,0:T(8,128)S(1)} %copy-done.31, ...), kind=kOutput, calls=%fused_computation.65 | convolution fusion | flops 2193620992 | bytes 27267088 | tf_op jit(solution)/shard_map/dot_general | solution.py:35
  458.7 11.3 %convolution_convert_fusion = bf16[2048,2048]{1,0:T(8,128)(2,1)} fusion(bf16[2048,1024]{1,0:T(8,128)(2,1)S(1)} %fusion.110, bf16[1024,2048]{1,0:T(8,128)(2,1)S(1)} %copy-done.74), kind=kOutput, calls=%fused_computation.4 | convolution fusion | flops 8594128896 | bytes 16777216 | tf_op jit(solution)/shard_map/dot_general | solution.py:35
  470.1 12.7 %convolution_convert_fusion.1 = bf16[1024,2048]{1,0:T(8,128)(2,1)S(1)} fusion(bf16[2048,1024]{1,0:T(8,128)(2,1)} %copy-done.27, bf16[2048,2048]{1,0:T(8,128)(2,1)} %all-gather.2.cloned.1.call-done), kind=kOutput, calls=%fused_computation.9 | convolution fusion | flops 8592031744 | bytes 16777216 | tf_op jit(solution)/shard_map/dot_general | solution.py:39
  485.9 11.5 %convolution_convert_fusion.2 = bf16[2048,1024]{1,0:T(8,128)(2,1)S(1)} fusion(bf16[2048,2048]{1,0:T(8,128)(2,1)} %copy-done.50, bf16[512,1024]{1,0:T(8,128)(2,1)S(1)} %copy-done.40, bf16[512,1024]{1,0:T(8,128)(2,1)S(1)} %copy-done.36, bf16[512,1024]{1,0:T(8,128)(2,1)S(1)} %copy-done.42, bf16[512,1024]{1,0:T(8,128)(2,1)S(1)} %copy-done.38), kind=kOutput, calls=%fused_computation.10 | convolution fusion | flops 8608808960 | bytes 16777216 | tf_op jit(solution)/shard_map/dot_general | solution.py:39
  502.4 6.1 collective-permute-done.78
  514.3 18.7 %collective-permute-done.70 = bf16[512,1024]{1,0:T(8,128)(2,1)S(1)} collective-permute-done((bf16[512,1024]{1,0:T(8,128)(2,1)S(1)}, bf16[512,1024]{1,0:T(8,128)(2,1)S(1)}, u32[]{:S(2)}, u32[]{:S(2)}) %collective-permute-start.70) | collective-permute-done | bytes 1048608 | tf_op jit(solution)/shard_map/ppermute | solution.py:329
  538.2 39.3 %collective-permute-done.31 = bf16[256,2048]{1,0:T(8,128)(2,1)S(1)} collective-permute-done((bf16[256,2048]{1,0:T(8,128)(2,1)S(1)}, bf16[256,2048]{1,0:T(8,128)(2,1)S(1)}, u32[]{:S(2)}, u32[]{:S(2)}) %collective-permute-start.31) | collective-permute-done | bytes 1048608 | tf_op jit(solution)/shard_map/ppermute | solution.py:224
  580.3 4.5 collective-permute-start.32
  585.7 6.7 collective-permute-done.71
  595.1 7.1 collective-permute-done.79
  610.2 22.8 %collective-permute-start.33 = (bf16[256,2048]{1,0:T(8,128)(2,1)S(1)}, bf16[256,2048]{1,0:T(8,128)(2,1)S(1)}, u32[]{:S(2)}, u32[]{:S(2)}) collective-permute-start(bf16[256,2048]{1,0:T(8,128)(2,1)S(1)} %get-tuple-element.95), channel_id=1, source_target_pairs={{0,2},{1,3},{2,4},{3,5},{4,6},{5,7},{8,10},{9,11},{10,12},{11,13},... | collective-permute-start | bytes 3145736 | tf_op jit(solution)/shard_map/ppermute | solution.py:224
  640.4 13.1 %collective-permute-done.33 = bf16[256,2048]{1,0:T(8,128)(2,1)S(1)} collective-permute-done((bf16[256,2048]{1,0:T(8,128)(2,1)S(1)}, bf16[256,2048]{1,0:T(8,128)(2,1)S(1)}, u32[]{:S(2)}, u32[]{:S(2)}) %collective-permute-start.33) | collective-permute-done | bytes 1048608 | tf_op jit(solution)/shard_map/ppermute | solution.py:224
  662.3 4.9 fusion.140
  668.7 4.6 collective-permute-start.37
  677.2 16.0 %collective-permute-done.77 = bf16[512,1024]{1,0:T(8,128)(2,1)} collective-permute-done((bf16[512,1024]{1,0:T(8,128)(2,1)}, bf16[512,1024]{1,0:T(8,128)(2,1)}, u32[]{:S(2)}, u32[]{:S(2)}) %collective-permute-start.77) | collective-permute-done | bytes 1048608 | tf_op jit(solution)/shard_map/ppermute | solution.py:334
  700.4 17.7 %collective-permute-done.41 = bf16[256,2048]{1,0:T(8,128)(2,1)S(1)} collective-permute-done((bf16[256,2048]{1,0:T(8,128)(2,1)S(1)}, bf16[256,2048]{1,0:T(8,128)(2,1)S(1)}, u32[]{:S(2)}, u32[]{:S(2)}) %collective-permute-start.41) | collective-permute-done | bytes 1048608 | tf_op jit(solution)/shard_map/ppermute | solution.py:224
  728.2 12.6 %collective-permute-done.43 = bf16[256,2048]{1,0:T(8,128)(2,1)S(1)} collective-permute-done((bf16[256,2048]{1,0:T(8,128)(2,1)S(1)}, bf16[256,2048]{1,0:T(8,128)(2,1)S(1)}, u32[]{:S(2)}, u32[]{:S(2)}) %collective-permute-start.43) | collective-permute-done | bytes 1048608 | tf_op jit(solution)/shard_map/ppermute | solution.py:224
  757.7 30.3 %attend_back.1 = bf16[2048,768]{1,0:T(8,128)(2,1)} custom-call(s32[64]{0:T(128)} %reshape.227.active, bf16[2048,768]{1,0:T(8,128)(2,1)} %pad_maximum_fusion.1.qkv, bf16[2048,256]{1,0:T(8,128)(2,1)} %pad_maximum_fusion.6.cot, f32[2048,256]{1,0:T(8,128)} %get-tuple-element.23.out_float, f32[2,8,2048]{2,1,0:T(8,128)} %get-tuple-element.24.log_total, ...), custom_call_target="tpu_custom_call" | custom-call | flops 5368709120 | bytes 9437184 | tf_op jit(solution)/shard_map/attend_back/pallas_call | solution.py:190
  800.3 5.9 convolution_convert_fusion.16
  806.2 7.6 convolution_convert_fusion.3
  825.6 16.7 %collective-permute-done.67 = bf16[32,2048]{1,0:T(8,128)(2,1)S(1)} collective-permute-done((bf16[32,2048]{1,0:T(8,128)(2,1)S(1)}, bf16[32,2048]{1,0:T(8,128)(2,1)S(1)}, u32[]{:S(2)}, u32[]{:S(2)}) %collective-permute-start.67) | collective-permute-done | bytes 131104 | tf_op jit(solution)/shard_map/ppermute | solution.py:329
  852.9 5.5 collective-permute-done.64
  858.7 6.2 collective-permute-done.69
  868.7 13.4 %collective-permute-done.59 = bf16[256,768]{1,0:T(8,128)(2,1)S(1)} collective-permute-done((bf16[256,768]{1,0:T(8,128)(2,1)S(1)}, bf16[256,768]{1,0:T(8,128)(2,1)S(1)}, u32[]{:S(2)}, u32[]{:S(2)}) %collective-permute-start.59) | collective-permute-done | bytes 393248 | tf_op jit(solution)/shard_map/ppermute | solution.py:329
  884.5 9.9 collective-permute-done.60
  895.3 8.8 collective-permute-done.56
  913.0 8.4 collective-permute-done.61
  923.4 9.5 collective-permute-done.50
  933.9 5.1 collective-permute-start.51
  945.9 13.6 %collective-permute-done.51 = bf16[256,2048]{1,0:T(8,128)(2,1)S(1)} collective-permute-done((bf16[256,2048]{1,0:T(8,128)(2,1)S(1)}, bf16[256,2048]{1,0:T(8,128)(2,1)S(1)}, u32[]{:S(2)}, u32[]{:S(2)}) %collective-permute-start.51) | collective-permute-done | bytes 1048608 | tf_op jit(solution)/shard_map/ppermute | solution.py:224
  959.5 9.5 collective-permute-done.53
  976.9 119.4 %all-reduce.3.cloned.1.call-done = (f32[6,2048]{1,0:T(8,128)}, f32[8,1792]{1,0:T(8,128)}) async-done(((f32[6,2048]{1,0:T(8,128)}, f32[8,1792]{1,0:T(8,128)}), (f32[6,2048]{1,0:T(8,128)}, f32[8,1792]{1,0:T(8,128)})) %all-reduce.3.cloned.1.call-update) | async-done | bytes 106512 | tf_op jit(solution)/shard_map/psum | solution.py:500
  (516 shorter events, 292.8 us)
Async XLA Ops:
  7.3 410.2 %all-gather.2.cloned.1.call-start = ((), (), s32[]{:S(2)}) async-start(), calls=%async_computation.2 | async-start | bytes 9437184 | tf_op jit(solution)/shard_map/all_gather | solution.py:432
  12.1 28.4 %collective-permute-start.2 = (bf16[256,2048]{1,0:T(8,128)(2,1)}, bf16[256,2048]{1,0:T(8,128)(2,1)}, u32[]{:S(2)}, u32[]{:S(2)}) collective-permute-start(bf16[256,2048]{1,0:T(8,128)(2,1)} %fusion.7), channel_id=1, source_target_pairs={{2,0},{3,1},{4,2},{5,3},{6,4},{7,5},{10,8},{11,9},{12,10},{13,11},... | collective-permute-start | bytes 3145736 | tf_op jit(solution)/shard_map/ppermute | solution.py:224
  13.4 28.4 %collective-permute-start.1 = (bf16[256,2048]{1,0:T(8,128)(2,1)}, bf16[256,2048]{1,0:T(8,128)(2,1)}, u32[]{:S(2)}, u32[]{:S(2)}) collective-permute-start(bf16[256,2048]{1,0:T(8,128)(2,1)} %fusion.7), channel_id=1, source_target_pairs={{0,2},{1,3},{2,4},{3,5},{4,6},{5,7},{8,10},{9,11},{10,12},{11,13},... | collective-permute-start | bytes 3145736 | tf_op jit(solution)/shard_map/ppermute | solution.py:224
  20.0 54.6 %collective-permute-start = (bf16[256,2048]{1,0:T(8,128)(2,1)}, bf16[256,2048]{1,0:T(8,128)(2,1)}, u32[]{:S(2)}, u32[]{:S(2)}) collective-permute-start(bf16[256,2048]{1,0:T(8,128)(2,1)} %fusion.7), channel_id=1, source_target_pairs={{0,1},{1,0},{2,3},{3,2},{4,5},{5,4},{6,7},{7,6},{8,9},{9,8},{10,11... | collective-permute-start | bytes 3145736 | tf_op jit(solution)/shard_map/ppermute | solution.py:227
  40.5 26.4 %collective-permute-start.5 = (bf16[256,2048]{1,0:T(8,128)(2,1)}, bf16[256,2048]{1,0:T(8,128)(2,1)S(1)}, u32[]{:S(2)}, u32[]{:S(2)}) collective-permute-start(bf16[256,2048]{1,0:T(8,128)(2,1)} %collective-permute-done.2), channel_id=1, source_target_pairs={{2,0},{3,1},{4,2},{5,3},{10,8},{11,9},{12,10},{13,11},{18,16},{19,... | collective-permute-start | bytes 3145736 | tf_op jit(solution)/shard_map/ppermute | solution.py:224
  41.8 25.1 %collective-permute-start.4 = (bf16[256,2048]{1,0:T(8,128)(2,1)}, bf16[256,2048]{1,0:T(8,128)(2,1)S(1)}, u32[]{:S(2)}, u32[]{:S(2)}) collective-permute-start(bf16[256,2048]{1,0:T(8,128)(2,1)} %collective-permute-done.1), channel_id=1, source_target_pairs={{2,4},{3,5},{4,6},{5,7},{10,12},{11,13},{12,14},{13,15},{18,20},{1... | collective-permute-start | bytes 3145736 | tf_op jit(solution)/shard_map/ppermute | solution.py:224
  69.0 25.7 %collective-permute-start.7 = (bf16[256,2048]{1,0:T(8,128)(2,1)}, bf16[256,2048]{1,0:T(8,128)(2,1)}, u32[]{:S(2)}, u32[]{:S(2)}) collective-permute-start(bf16[256,2048]{1,0:T(8,128)(2,1)} %broadcast_select_fusion.14), channel_id=1, source_target_pairs={{4,6},{5,7},{2,0},{3,1},{12,14},{13,15},{10,8},{11,9},{20,22},{21,... | collective-permute-start | bytes 3145736 | tf_op jit(solution)/shard_map/ppermute | solution.py:224
  163.9 30.0 %collective-permute-start.11 = (bf16[256,2048]{1,0:T(8,128)(2,1)}, bf16[256,2048]{1,0:T(8,128)(2,1)}, u32[]{:S(2)}, u32[]{:S(2)}) collective-permute-start(bf16[256,2048]{1,0:T(8,128)(2,1)} %broadcast_select_fusion.43), channel_id=1, source_target_pairs={{0,1},{1,0},{2,3},{3,2},{4,5},{5,4},{6,7},{7,6},{8,9},{9,8},{10,11... | collective-permute-start | bytes 3145736 | tf_op jit(solution)/shard_map/ppermute | solution.py:227
  184.1 38.5 %collective-permute-start.14 = (bf16[256,2048]{1,0:T(8,128)(2,1)}, bf16[256,2048]{1,0:T(8,128)(2,1)}, u32[]{:S(2)}, u32[]{:S(2)}) collective-permute-start(bf16[256,2048]{1,0:T(8,128)(2,1)} %get-tuple-element.103), channel_id=1, source_target_pairs={{0,2},{1,3},{2,4},{3,5},{8,10},{9,11},{10,12},{11,13},{16,18},{17,... | collective-permute-start | bytes 3145736 | tf_op jit(solution)/shard_map/ppermute | solution.py:224
  191.0 471.2 %reduce-scatter.2.cloned.1.call-start = ((), (), s32[]{:S(2)}) async-start(), calls=%async_computation.1 | async-start | bytes 9437184 | tf_op jit(solution)/shard_map/reduce_scatter | solution.py:457
  192.8 58.8 %collective-permute-start.16 = (bf16[256,2048]{1,0:T(8,128)(2,1)}, bf16[256,2048]{1,0:T(8,128)(2,1)S(1)}, u32[]{:S(2)}, u32[]{:S(2)}) collective-permute-start(bf16[256,2048]{1,0:T(8,128)(2,1)} %get-tuple-element.103), channel_id=1, source_target_pairs={{4,2},{5,3},{6,4},{7,5},{12,10},{13,11},{14,12},{15,13},{20,18},{2... | collective-permute-start | bytes 3145736 | tf_op jit(solution)/shard_map/ppermute | solution.py:224
  193.8 60.1 %collective-permute-start.9 = (bf16[256,2048]{1,0:T(8,128)(2,1)S(1)}, bf16[256,2048]{1,0:T(8,128)(2,1)S(1)}, u32[]{:S(2)}, u32[]{:S(2)}) collective-permute-start(bf16[256,2048]{1,0:T(8,128)(2,1)S(1)} %broadcast_select_fusion.45), channel_id=1, source_target_pairs={{0,1},{1,0},{2,3},{3,2},{4,5},{5,4},{6,7},{7,6},{8,9},{9,8},{10,11... | collective-permute-start | bytes 3145736 | tf_op jit(solution)/shard_map/ppermute | solution.py:227
  225.2 69.6 %collective-permute-start.15 = (bf16[256,2048]{1,0:T(8,128)(2,1)S(1)}, bf16[256,2048]{1,0:T(8,128)(2,1)S(1)}, u32[]{:S(2)}, u32[]{:S(2)}) collective-permute-start(bf16[256,2048]{1,0:T(8,128)(2,1)S(1)} %get-tuple-element.101), channel_id=1, source_target_pairs={{0,2},{1,3},{2,4},{3,5},{4,6},{5,7},{8,10},{9,11},{10,12},{11,13},... | collective-permute-start | bytes 3145736 | tf_op jit(solution)/shard_map/ppermute | solution.py:224
  252.1 50.4 %collective-permute-start.17 = (bf16[256,2048]{1,0:T(8,128)(2,1)S(1)}, bf16[256,2048]{1,0:T(8,128)(2,1)S(1)}, u32[]{:S(2)}, u32[]{:S(2)}) collective-permute-start(bf16[256,2048]{1,0:T(8,128)(2,1)S(1)} %add_convert_fusion.19), channel_id=1, source_target_pairs={{2,0},{3,1},{4,2},{5,3},{6,4},{7,5},{10,8},{11,9},{12,10},{13,11},... | collective-permute-start | bytes 3145736 | tf_op jit(solution)/shard_map/ppermute | solution.py:224
  305.8 34.2 %collective-permute-start.20 = (bf16[256,2048]{1,0:T(8,128)(2,1)}, bf16[256,2048]{1,0:T(8,128)(2,1)S(1)}, u32[]{:S(2)}, u32[]{:S(2)}) collective-permute-start(bf16[256,2048]{1,0:T(8,128)(2,1)} %add_convert_fusion.18), channel_id=1, source_target_pairs={{2,0},{3,1},{4,2},{5,3},{6,4},{7,5},{10,8},{11,9},{12,10},{13,11},... | collective-permute-start | bytes 3145736 | tf_op jit(solution)/shard_map/ppermute | solution.py:224
  307.1 34.2 %collective-permute-start.19 = (bf16[256,2048]{1,0:T(8,128)(2,1)}, bf16[256,2048]{1,0:T(8,128)(2,1)S(1)}, u32[]{:S(2)}, u32[]{:S(2)}) collective-permute-start(bf16[256,2048]{1,0:T(8,128)(2,1)} %add_convert_fusion.18), channel_id=1, source_target_pairs={{0,2},{1,3},{2,4},{3,5},{4,6},{5,7},{8,10},{9,11},{10,12},{11,13},... | collective-permute-start | bytes 3145736 | tf_op jit(solution)/shard_map/ppermute | solution.py:224
  368.2 25.7 %collective-permute-start.18 = (bf16[256,2048]{1,0:T(8,128)(2,1)}, bf16[256,2048]{1,0:T(8,128)(2,1)}, u32[]{:S(2)}, u32[]{:S(2)}) collective-permute-start(bf16[256,2048]{1,0:T(8,128)(2,1)} %add_convert_fusion.18), channel_id=1, source_target_pairs={{0,1},{1,0},{2,3},{3,2},{4,5},{5,4},{6,7},{7,6},{8,9},{9,8},{10,11... | collective-permute-start | bytes 3145736 | tf_op jit(solution)/shard_map/ppermute | solution.py:227
  457.9 182.1 %collective-permute-start.27 = (bf16[256,2048]{1,0:T(8,128)(2,1)}, bf16[256,2048]{1,0:T(8,128)(2,1)}, u32[]{:S(2)}, u32[]{:S(2)}) collective-permute-start(bf16[256,2048]{1,0:T(8,128)(2,1)} %broadcast_select_fusion.33), channel_id=1, source_target_pairs={{0,1},{1,0},{2,3},{3,2},{4,5},{5,4},{6,7},{7,6},{8,9},{9,8},{10,11... | collective-permute-start | bytes 3145736 | tf_op jit(solution)/shard_map/ppermute | solution.py:227
  458.2 145.8 %collective-permute-start.29 = (bf16[256,2048]{1,0:T(8,128)(2,1)}, bf16[256,2048]{1,0:T(8,128)(2,1)}, u32[]{:S(2)}, u32[]{:S(2)}) collective-permute-start(bf16[256,2048]{1,0:T(8,128)(2,1)} %broadcast_select_fusion.31), channel_id=1, source_target_pairs={{0,1},{1,0},{2,3},{3,2},{4,5},{5,4},{6,7},{7,6},{8,9},{9,8},{10,11... | collective-permute-start | bytes 3145736 | tf_op jit(solution)/shard_map/ppermute | solution.py:227
  458.4 54.1 %collective-permute-start.30 = (bf16[256,2048]{1,0:T(8,128)(2,1)}, bf16[256,2048]{1,0:T(8,128)(2,1)}, u32[]{:S(2)}, u32[]{:S(2)}) collective-permute-start(bf16[256,2048]{1,0:T(8,128)(2,1)} %broadcast_select_fusion.30), channel_id=1, source_target_pairs={{0,1},{1,0},{2,3},{3,2},{4,5},{5,4},{6,7},{7,6},{8,9},{9,8},{10,11... | collective-permute-start | bytes 3145736 | tf_op jit(solution)/shard_map/ppermute | solution.py:227
  470.1 626.2 %all-reduce.3.cloned.1.call-start = ((), (), s32[]{:S(2)}) async-start(), calls=%async_computation.3 | async-start | bytes 245760 | tf_op jit(solution)/shard_map/psum | solution.py:500
  483.1 25.4 %collective-permute-start.78 = (bf16[256,2048]{1,0:T(8,128)(2,1)S(1)}, bf16[256,2048]{1,0:T(8,128)(2,1)S(1)}, u32[]{:S(2)}, u32[]{:S(2)}) collective-permute-start(bf16[256,2048]{1,0:T(8,128)(2,1)S(1)} %get-tuple-element.117), channel_id=1, source_target_pairs={{0,8},{8,0},{16,24},{24,16},{1,9},{9,1},{17,25},{25,17},{2,10},{10... | collective-permute-start | bytes 3145736 | tf_op jit(solution)/shard_map/ppermute | solution.py:329
  483.1 26.0 %collective-permute-start.82 = (bf16[256,2048]{1,0:T(8,128)(2,1)S(1)}, bf16[256,2048]{1,0:T(8,128)(2,1)S(1)}, u32[]{:S(2)}, u32[]{:S(2)}) collective-permute-start(bf16[256,2048]{1,0:T(8,128)(2,1)S(1)} %get-tuple-element.118), channel_id=1, source_target_pairs={{0,16},{8,24},{16,0},{24,8},{1,17},{9,25},{17,1},{25,9},{2,18},{10... | collective-permute-start | bytes 3145736 | tf_op jit(solution)/shard_map/ppermute | solution.py:329
  509.1 25.2 %collective-permute-start.74 = (bf16[512,1024]{1,0:T(8,128)(2,1)S(1)}, bf16[512,1024]{1,0:T(8,128)(2,1)S(1)}, u32[]{:S(2)}, u32[]{:S(2)}) collective-permute-start(bf16[512,1024]{1,0:T(8,128)(2,1)S(1)} %get-tuple-element.122), channel_id=1, source_target_pairs={{0,16},{8,24},{16,0},{24,8},{1,17},{9,25},{17,1},{25,9},{2,18},{10... | collective-permute-start | bytes 3145736 | tf_op jit(solution)/shard_map/ppermute | solution.py:329
  533.0 44.5 %collective-permute-start.31 = (bf16[256,2048]{1,0:T(8,128)(2,1)S(1)}, bf16[256,2048]{1,0:T(8,128)(2,1)S(1)}, u32[]{:S(2)}, u32[]{:S(2)}) collective-permute-start(bf16[256,2048]{1,0:T(8,128)(2,1)S(1)} %add_convert_fusion.14), channel_id=1, source_target_pairs={{0,2},{1,3},{6,4},{7,5},{8,10},{9,11},{14,12},{15,13},{16,18},{17,... | collective-permute-start | bytes 3145736 | tf_op jit(solution)/shard_map/ppermute | solution.py:224
  534.4 45.9 %collective-permute-start.83 = (bf16[128,2048]{1,0:T(8,128)(2,1)S(1)}, bf16[128,2048]{1,0:T(8,128)(2,1)S(1)}, u32[]{:S(2)}, u32[]{:S(2)}) collective-permute-start(bf16[128,2048]{1,0:T(8,128)(2,1)S(1)} %broadcast_select_fusion.62), channel_id=1, source_target_pairs={{0,8},{8,0},{16,24},{24,16},{1,9},{9,1},{17,25},{25,17},{2,10},{10... | collective-permute-start | bytes 1572872 | tf_op jit(solution)/shard_map/ppermute | solution.py:329
  536.7 48.3 %collective-permute-start.75 = (bf16[256,1024]{1,0:T(8,128)(2,1)S(1)}, bf16[256,1024]{1,0:T(8,128)(2,1)S(1)}, u32[]{:S(2)}, u32[]{:S(2)}) collective-permute-start(bf16[256,1024]{1,0:T(8,128)(2,1)S(1)} %broadcast_select_fusion.68), channel_id=1, source_target_pairs={{0,8},{8,0},{16,24},{24,16},{1,9},{9,1},{17,25},{25,17},{2,10},{10... | collective-permute-start | bytes 1572872 | tf_op jit(solution)/shard_map/ppermute | solution.py:329
  580.3 26.3 %collective-permute-start.32 = (bf16[256,2048]{1,0:T(8,128)(2,1)S(1)}, bf16[256,2048]{1,0:T(8,128)(2,1)S(1)}, u32[]{:S(2)}, u32[]{:S(2)}) collective-permute-start(bf16[256,2048]{1,0:T(8,128)(2,1)S(1)} %get-tuple-element.97), channel_id=1, source_target_pairs={{0,2},{1,3},{2,4},{3,5},{8,10},{9,11},{10,12},{11,13},{16,18},{17,... | collective-permute-start | bytes 3145736 | tf_op jit(solution)/shard_map/ppermute | solution.py:224
  592.4 43.9 %collective-permute-start.84 = (bf16[128,2048]{1,0:T(8,128)(2,1)S(1)}, bf16[128,2048]{1,0:T(8,128)(2,1)S(1)}, u32[]{:S(2)}, u32[]{:S(2)}) collective-permute-start(bf16[128,2048]{1,0:T(8,128)(2,1)S(1)} %add_convert_fusion.32), channel_id=1, source_target_pairs={{0,8},{8,0},{16,24},{24,16},{1,9},{9,1},{17,25},{25,17},{2,10},{10... | collective-permute-start | bytes 1572872 | tf_op jit(solution)/shard_map/ppermute | solution.py:334
  604.0 70.7 %collective-permute-start.80 = (bf16[128,2048]{1,0:T(8,128)(2,1)}, bf16[128,2048]{1,0:T(8,128)(2,1)}, u32[]{:S(2)}, u32[]{:S(2)}) collective-permute-start(bf16[128,2048]{1,0:T(8,128)(2,1)} %add_convert_fusion.33), channel_id=1, source_target_pairs={{0,16},{8,24},{16,0},{24,8},{1,17},{9,25},{17,1},{25,9},{2,18},{10... | collective-permute-start | bytes 1572872 | tf_op jit(solution)/shard_map/ppermute | solution.py:334
  606.6 27.0 %collective-permute-start.76 = (bf16[256,1024]{1,0:T(8,128)(2,1)S(1)}, bf16[256,1024]{1,0:T(8,128)(2,1)S(1)}, u32[]{:S(2)}, u32[]{:S(2)}) collective-permute-start(bf16[256,1024]{1,0:T(8,128)(2,1)S(1)} %add_convert_fusion.34), channel_id=1, source_target_pairs={{0,8},{8,0},{16,24},{24,16},{1,9},{9,1},{17,25},{25,17},{2,10},{10... | collective-permute-start | bytes 1572872 | tf_op jit(solution)/shard_map/ppermute | solution.py:334
  610.2 43.4 %collective-permute-start.33 = (bf16[256,2048]{1,0:T(8,128)(2,1)S(1)}, bf16[256,2048]{1,0:T(8,128)(2,1)S(1)}, u32[]{:S(2)}, u32[]{:S(2)}) collective-permute-start(bf16[256,2048]{1,0:T(8,128)(2,1)S(1)} %get-tuple-element.95), channel_id=1, source_target_pairs={{0,2},{1,3},{2,4},{3,5},{4,6},{5,7},{8,10},{9,11},{10,12},{11,13},... | collective-permute-start | bytes 3145736 | tf_op jit(solution)/shard_map/ppermute | solution.py:224
  636.3 32.4 %collective-permute-start.72 = (bf16[256,1024]{1,0:T(8,128)(2,1)}, bf16[256,1024]{1,0:T(8,128)(2,1)}, u32[]{:S(2)}, u32[]{:S(2)}) collective-permute-start(bf16[256,1024]{1,0:T(8,128)(2,1)} %add_convert_fusion.35), channel_id=1, source_target_pairs={{0,16},{8,24},{16,0},{24,8},{1,17},{9,25},{17,1},{25,9},{2,18},{10... | collective-permute-start | bytes 1572872 | tf_op jit(solution)/shard_map/ppermute | solution.py:334
  640.0 58.1 %collective-permute-start.85 = (bf16[256,2048]{1,0:T(8,128)(2,1)}, bf16[256,2048]{1,0:T(8,128)(2,1)}, u32[]{:S(2)}, u32[]{:S(2)}) collective-permute-start(bf16[256,2048]{1,0:T(8,128)(2,1)} %pad_maximum_fusion.10), channel_id=1, source_target_pairs={{0,16},{8,24},{16,0},{24,8},{1,17},{9,25},{17,1},{25,9},{2,18},{10... | collective-permute-start | bytes 3145736 | tf_op jit(solution)/shard_map/ppermute | solution.py:334
  653.5 39.7 %collective-permute-start.77 = (bf16[512,1024]{1,0:T(8,128)(2,1)}, bf16[512,1024]{1,0:T(8,128)(2,1)}, u32[]{:S(2)}, u32[]{:S(2)}) collective-permute-start(bf16[512,1024]{1,0:T(8,128)(2,1)} %pad_maximum_fusion.8), channel_id=1, source_target_pairs={{0,16},{8,24},{16,0},{24,8},{1,17},{9,25},{17,1},{25,9},{2,18},{10... | collective-permute-start | bytes 3145736 | tf_op jit(solution)/shard_map/ppermute | solution.py:334
  667.4 26.9 %collective-permute-start.38 = (bf16[256,2048]{1,0:T(8,128)(2,1)S(1)}, bf16[256,2048]{1,0:T(8,128)(2,1)S(1)}, u32[]{:S(2)}, u32[]{:S(2)}) collective-permute-start(bf16[256,2048]{1,0:T(8,128)(2,1)S(1)} %convert_element_type.590), channel_id=1, source_target_pairs={{2,0},{3,1},{4,2},{5,3},{6,4},{7,5},{10,8},{11,9},{12,10},{13,11},... | collective-permute-start | bytes 3145736 | tf_op jit(solution)/shard_map/ppermute | solution.py:224
  668.7 26.9 %collective-permute-start.37 = (bf16[256,2048]{1,0:T(8,128)(2,1)S(1)}, bf16[256,2048]{1,0:T(8,128)(2,1)S(1)}, u32[]{:S(2)}, u32[]{:S(2)}) collective-permute-start(bf16[256,2048]{1,0:T(8,128)(2,1)S(1)} %convert_element_type.590), channel_id=1, source_target_pairs={{0,2},{1,3},{2,4},{3,5},{4,6},{5,7},{8,10},{9,11},{10,12},{11,13},... | collective-permute-start | bytes 3145736 | tf_op jit(solution)/shard_map/ppermute | solution.py:224
  674.7 25.1 %collective-permute-start.73 = (bf16[512,1024]{1,0:T(8,128)(2,1)S(1)}, bf16[512,1024]{1,0:T(8,128)(2,1)S(1)}, u32[]{:S(2)}, u32[]{:S(2)}) collective-permute-start(bf16[512,1024]{1,0:T(8,128)(2,1)S(1)} %pad_maximum_fusion.7), channel_id=1, source_target_pairs={{0,8},{8,0},{16,24},{24,16},{1,9},{9,1},{17,25},{25,17},{2,10},{10... | collective-permute-start | bytes 3145736 | tf_op jit(solution)/shard_map/ppermute | solution.py:334
  693.2 30.6 %collective-permute-start.81 = (bf16[256,2048]{1,0:T(8,128)(2,1)S(1)}, bf16[256,2048]{1,0:T(8,128)(2,1)S(1)}, u32[]{:S(2)}, u32[]{:S(2)}) collective-permute-start(bf16[256,2048]{1,0:T(8,128)(2,1)S(1)} %pad_maximum_fusion.9), channel_id=1, source_target_pairs={{0,8},{8,0},{16,24},{24,16},{1,9},{9,1},{17,25},{25,17},{2,10},{10... | collective-permute-start | bytes 3145736 | tf_op jit(solution)/shard_map/ppermute | solution.py:334
  816.4 48.6 %collective-permute-start.54 = (bf16[512,768]{1,0:T(8,128)(2,1)S(1)}, bf16[512,768]{1,0:T(8,128)(2,1)S(1)}, u32[]{:S(2)}, u32[]{:S(2)}) collective-permute-start(bf16[512,768]{1,0:T(8,128)(2,1)S(1)} %get-tuple-element.125), channel_id=1, source_target_pairs={{0,8},{8,0},{16,24},{24,16},{1,9},{9,1},{17,25},{25,17},{2,10},{10... | collective-permute-start | bytes 2359304 | tf_op jit(solution)/shard_map/ppermute | solution.py:329
  816.5 48.7 %collective-permute-start.58 = (bf16[512,768]{1,0:T(8,128)(2,1)S(1)}, bf16[512,768]{1,0:T(8,128)(2,1)S(1)}, u32[]{:S(2)}, u32[]{:S(2)}) collective-permute-start(bf16[512,768]{1,0:T(8,128)(2,1)S(1)} %get-tuple-element.126), channel_id=1, source_target_pairs={{0,16},{8,24},{16,0},{24,8},{1,17},{9,25},{17,1},{25,9},{2,18},{10... | collective-permute-start | bytes 2359304 | tf_op jit(solution)/shard_map/ppermute | solution.py:329
  818.4 49.5 %collective-permute-start.48 = (bf16[256,2048]{1,0:T(8,128)(2,1)S(1)}, bf16[256,2048]{1,0:T(8,128)(2,1)S(1)}, u32[]{:S(2)}, u32[]{:S(2)}) collective-permute-start(bf16[256,2048]{1,0:T(8,128)(2,1)S(1)} %broadcast_select_fusion.18), channel_id=1, source_target_pairs={{0,1},{1,0},{2,3},{3,2},{4,5},{5,4},{6,7},{7,6},{8,9},{9,8},{10,11... | collective-permute-start | bytes 3145736 | tf_op jit(solution)/shard_map/ppermute | solution.py:227
  823.2 100.2 %collective-permute-start.47 = (bf16[256,2048]{1,0:T(8,128)(2,1)S(1)}, bf16[256,2048]{1,0:T(8,128)(2,1)S(1)}, u32[]{:S(2)}, u32[]{:S(2)}) collective-permute-start(bf16[256,2048]{1,0:T(8,128)(2,1)S(1)} %broadcast_select_fusion.19), channel_id=1, source_target_pairs={{0,1},{1,0},{2,3},{3,2},{4,5},{5,4},{6,7},{7,6},{8,9},{9,8},{10,11... | collective-permute-start | bytes 3145736 | tf_op jit(solution)/shard_map/ppermute | solution.py:227
  864.9 40.4 %collective-permute-start.46 = (bf16[256,2048]{1,0:T(8,128)(2,1)S(1)}, bf16[256,2048]{1,0:T(8,128)(2,1)S(1)}, u32[]{:S(2)}, u32[]{:S(2)}) collective-permute-start(bf16[256,2048]{1,0:T(8,128)(2,1)S(1)} %broadcast_select_fusion.20), channel_id=1, source_target_pairs={{0,1},{1,0},{2,3},{3,2},{4,5},{5,4},{6,7},{7,6},{8,9},{9,8},{10,11... | collective-permute-start | bytes 3145736 | tf_op jit(solution)/shard_map/ppermute | solution.py:227
  884.3 61.6 %collective-permute-start.45 = (bf16[256,2048]{1,0:T(8,128)(2,1)S(1)}, bf16[256,2048]{1,0:T(8,128)(2,1)S(1)}, u32[]{:S(2)}, u32[]{:S(2)}) collective-permute-start(bf16[256,2048]{1,0:T(8,128)(2,1)S(1)} %broadcast_select_fusion.21), channel_id=1, source_target_pairs={{0,1},{1,0},{2,3},{3,2},{4,5},{5,4},{6,7},{7,6},{8,9},{9,8},{10,11... | collective-permute-start | bytes 3145736 | tf_op jit(solution)/shard_map/ppermute | solution.py:227
  907.5 25.4 %collective-permute-start.50 = (bf16[256,2048]{1,0:T(8,128)(2,1)S(1)}, bf16[256,2048]{1,0:T(8,128)(2,1)S(1)}, u32[]{:S(2)}, u32[]{:S(2)}) collective-permute-start(bf16[256,2048]{1,0:T(8,128)(2,1)S(1)} %get-tuple-element.92), channel_id=1, source_target_pairs={{0,2},{1,3},{2,4},{3,5},{8,10},{9,11},{10,12},{11,13},{16,18},{17,... | collective-permute-start | bytes 3145736 | tf_op jit(solution)/shard_map/ppermute | solution.py:224
  933.9 25.6 %collective-permute-start.51 = (bf16[256,2048]{1,0:T(8,128)(2,1)S(1)}, bf16[256,2048]{1,0:T(8,128)(2,1)S(1)}, u32[]{:S(2)}, u32[]{:S(2)}) collective-permute-start(bf16[256,2048]{1,0:T(8,128)(2,1)S(1)} %get-tuple-element.90), channel_id=1, source_target_pairs={{0,2},{1,3},{2,4},{3,5},{4,6},{5,7},{8,10},{9,11},{10,12},{11,13},... | collective-permute-start | bytes 3145736 | tf_op jit(solution)/shard_map/ppermute | solution.py:224
  939.6 29.4 %collective-permute-start.53 = (bf16[256,2048]{1,0:T(8,128)(2,1)S(1)}, bf16[256,2048]{1,0:T(8,128)(2,1)S(1)}, u32[]{:S(2)}, u32[]{:S(2)}) collective-permute-start(bf16[256,2048]{1,0:T(8,128)(2,1)S(1)} %add_convert_fusion.4), channel_id=1, source_target_pairs={{2,0},{3,1},{4,2},{5,3},{6,4},{7,5},{10,8},{11,9},{12,10},{13,11},... | collective-permute-start | bytes 3145736 | tf_op jit(solution)/shard_map/ppermute | solution.py:224
  (123 other events, 2186.9 us)
Sparse Core Ops, SparseCore 0:
  191.2 111.3 all-gather.1
  470.2 110.9 reduce-scatter.1
  972.7 123.5 all-reduce.2
